TPU v7x, 128 devices: a whole 4x4x4 slice. The times are simulated.
128 devices in a mesh: row: 2 (over y_lo), col: 16 (over x, y_hi, core), mode: 4 (over z).
Axes of the slice: x: 4, y: 4 (y_hi: 2, y_lo: 2; y = y_hi * 2 + y_lo), z: 4, core: 2. Of those that a mesh axis runs over, the one named last changes fastest.
Arguments:
- object_slab: float32 [2, 4096, 4096], P(None, 'row', 'col'), may hold values from -4.2 to 4.2
- probe_modes: float32 [2, 4, 256, 256], P(None, 'mode'), may hold values from -4.2 to 4.2
- amplitudes: float32 [512, 256, 256], P(('row', 'col')), may hold values from 0.5 to 3.5
- scan_counts: int32 [32], replicated, may hold values from 1 to 16, as said below
- scan_positions: int32 [2, 512], P(None, ('row', 'col')), may hold values from 0 to 3840, as said below
Outputs:
- object_grad: float32 [2, 4096, 4096], P(None, 'row', 'col')
- probe_grad: float32 [2, 4, 256, 256], P(None, 'mode')
- position_grad: float32 [2, 512], P(None, ('row', 'col'))
Inputs may be any that keep to these rules, and one draw needn't show every extreme that they name: `scan_counts`: each tile holds between 1 and 16 patterns, and some tile holds exactly 16; a tile's active slots are its first ones. `scan_positions`: every slot's window starts inside the tile that owns the slot (slot p is owned by tile p // 16, tiles numbered row index * 16 + column index) and lies wholly inside the object; inactive slots also carry such positions.
All inputs are finite; a program needn't handle non-finite values.
Results may differ from a plain program's by a relative error of at most 0.0003.
Values sent between devices are 32-bit elements; how exact they have to be, the bound alone decides.
A program may use at most 128 MiB of HBM per device.

v0:
```python
import math

import jax
import jax.numpy as jnp
from jax import lax
from jax.sharding import PartitionSpec as P

HIGHEST = lax.Precision.HIGHEST


def passed_along(x, axis, by):
    peers = lax.axis_size(axis)
    pairs = [(i, i + by) for i in range(peers) if 0 <= i + by < peers]
    return lax.ppermute(x, axis, pairs)


def dft_tables(window):
    counter = lax.iota(jnp.int32, window)
    product = counter[:, None] * counter[None, :] % window
    angle = product.astype(jnp.float32) * (2.0 * math.pi / window)
    factor_norm = 1.0 / math.sqrt(window)
    return (jnp.cos(angle) * factor_norm, jnp.sin(angle) * factor_norm)


def left_apply(table, field):
    return jnp.einsum("kn,bmnj->bmkj", table, field, precision=HIGHEST)


def right_apply(field, table):
    return jnp.einsum("bmkn,nj->bmkj", field, table, precision=HIGHEST)


def per_device(object_slab, probe_modes, amplitudes, scan_counts, scan_positions):
    window = probe_modes.shape[-1]
    tile_rows = object_slab.shape[1]
    tile_cols = object_slab.shape[2]
    slots = amplitudes.shape[0]
    per_block = 4
    right_strip = passed_along(object_slab, "col", -1)
    widened = jnp.concatenate([object_slab, right_strip], axis=2)
    lower_strip = passed_along(widened[:, :window, :], "row", -1)
    extended = jnp.concatenate([widened, lower_strip], axis=1)
    rows_at = scan_positions[0] - lax.axis_index("row") * tile_rows
    cols_at = scan_positions[1] - lax.axis_index("col") * tile_cols
    cosine, sine = dft_tables(window)
    probe_re = probe_modes[0][None]
    probe_im = probe_modes[1][None]
    col_count = lax.axis_size("col")
    tile_here = lax.axis_index("row") * col_count + lax.axis_index("col")
    own_count = scan_counts[tile_here]

    def cut_windows(rows_list, cols_list):
        return jax.vmap(
            lambda row_at, col_at: lax.dynamic_slice(
                extended, (0, row_at, col_at), (2, window, window)
            )
        )(rows_list, cols_list)

    def transform(windows, measured, active_blk):
        obj_re = windows[:, 0][:, None]
        obj_im = windows[:, 1][:, None]
        wave_re = probe_re * obj_re - probe_im * obj_im
        wave_im = probe_re * obj_im + probe_im * obj_re
        half_re = left_apply(cosine, wave_re) + left_apply(sine, wave_im)
        half_im = left_apply(cosine, wave_im) - left_apply(sine, wave_re)
        far_re = right_apply(half_re, cosine) + right_apply(half_im, sine)
        far_im = right_apply(half_im, cosine) - right_apply(half_re, sine)
        partial_int = jnp.sum(far_re * far_re + far_im * far_im, axis=1)
        intensity = lax.psum(partial_int, "mode")
        factor = 0.25 * (1.0 - measured / jnp.sqrt(intensity + 0.5)) * active_blk
        back_re = factor[:, None] * far_re
        back_im = factor[:, None] * far_im
        mid_re = left_apply(cosine, back_re) - left_apply(sine, back_im)
        mid_im = left_apply(cosine, back_im) + left_apply(sine, back_re)
        near_re = right_apply(mid_re, cosine) - right_apply(mid_im, sine)
        near_im = right_apply(mid_im, cosine) + right_apply(mid_re, sine)
        gobj_re = jnp.sum(probe_re * near_re + probe_im * near_im, axis=1)
        gobj_im = jnp.sum(probe_re * near_im - probe_im * near_re, axis=1)
        gprobe_re = jnp.sum(obj_re * near_re + obj_im * near_im, axis=0)
        gprobe_im = jnp.sum(obj_re * near_im - obj_im * near_re, axis=0)
        win_re = windows[:, 0]
        win_im = windows[:, 1]
        drow_re = (win_re[:, 2:, :] - win_re[:, :-2, :]) * 0.5
        drow_im = (win_im[:, 2:, :] - win_im[:, :-2, :]) * 0.5
        dcol_re = (win_re[:, :, 2:] - win_re[:, :, :-2]) * 0.5
        dcol_im = (win_im[:, :, 2:] - win_im[:, :, :-2]) * 0.5
        along_rows = (
            jnp.sum(gobj_re[:, 1:-1, :] * drow_re + gobj_im[:, 1:-1, :] * drow_im, axis=(1, 2))
            / window
        )
        along_cols = (
            jnp.sum(gobj_re[:, :, 1:-1] * dcol_re + gobj_im[:, :, 1:-1] * dcol_im, axis=(1, 2))
            / window
        )
        pieces = jnp.stack([gobj_re, gobj_im], axis=1)
        return (pieces, jnp.stack([along_rows, along_cols]), jnp.stack([gprobe_re, gprobe_im]))

    def advance(index, totals):
        grad_ext, grad_probe, shift_grads = totals
        start_slot = index * per_block
        rows_blk = lax.dynamic_slice_in_dim(rows_at, start_slot, per_block)
        cols_blk = lax.dynamic_slice_in_dim(cols_at, start_slot, per_block)
        slot_ids = start_slot + lax.iota(jnp.int32, per_block)
        active_blk = (slot_ids < own_count).astype(jnp.float32)[:, None, None]
        measured = lax.dynamic_slice_in_dim(amplitudes, start_slot, per_block, 0)
        windows = cut_windows(rows_blk, cols_blk)
        pieces, along, gprobe = transform(windows, measured, active_blk)
        grad_probe = grad_probe + gprobe
        shift_grads = lax.dynamic_update_slice_in_dim(shift_grads, along, start_slot, 1)

        def deposit(slot, total):
            region = lax.dynamic_slice(
                total, (0, rows_blk[slot], cols_blk[slot]), (2, window, window)
            )
            return lax.dynamic_update_slice(
                total, region + pieces[slot], (0, rows_blk[slot], cols_blk[slot])
            )

        grad_ext = lax.fori_loop(0, per_block, deposit, grad_ext)
        return (grad_ext, grad_probe, shift_grads)

    initial = (
        jnp.zeros_like(extended),
        jnp.zeros_like(probe_modes),
        jnp.zeros((2, slots), jnp.float32),
    )
    grad_ext, grad_probe, shift_grads = lax.fori_loop(0, slots // per_block, advance, initial)
    lower_back = passed_along(grad_ext[:, tile_rows:, :], "row", 1)
    grad_ext = grad_ext[:, :tile_rows, :].at[:, :window, :].add(lower_back)
    right_back = passed_along(grad_ext[:, :, tile_cols:], "col", 1)
    grad_tile = grad_ext[:, :, :tile_cols].at[:, :, :window].add(right_back)
    grad_tile, shift_total = lax.psum((grad_tile, shift_grads), "mode")
    probe_total = lax.psum(grad_probe, ("row", "col")) / 16.0
    return (grad_tile, probe_total, shift_total)


def solution(mesh):
    in_specs = (
        P(None, "row", "col"),
        P(None, "mode", None, None),
        P(("row", "col"), None, None),
        P(),
        P(None, ("row", "col")),
    )
    out_specs = (P(None, "row", "col"), P(None, "mode", None, None), P(None, ("row", "col")))
    return jax.shard_map(
        per_device, mesh=mesh, in_specs=in_specs, out_specs=out_specs, check_vma=False
    )
```

profile of v0, /device:TPU:10, one launch (start us, length us, event | category | flops | bytes accessed | tf_op | source)
XLA Modules:
  0.0 1055.9 jit_solution(12943325170141575407)
XLA Ops:
  14.5 43.5 %collective-permute-done = f32[2,2048,256]{2,1,0:T(8,128)S(1)} collective-permute-done((f32[2,2048,256]{2,1,0:T(8,128)}, f32[2,2048,256]{2,1,0:T(8,128)S(1)}, u32[]{:S(2)}, u32[]{:S(2)}) %collective-permute-start) | collective-permute-done | bytes 4194336 | tf_op jit(solution)/shard_map/ppermute | solution.py:14
  66.9 21.9 %collective-permute-done.1 = f32[2,256,512]{2,1,0:T(8,128)S(1)} collective-permute-done((f32[2,256,512]{2,1,0:T(8,128)S(1)}, f32[2,256,512]{2,1,0:T(8,128)S(1)}, u32[]{:S(2)}, u32[]{:S(2)}) %collective-permute-start.1) | collective-permute-done | bytes 1048608 | tf_op jit(solution)/shard_map/ppermute | solution.py:14
  88.8 8.1 pad_maximum_fusion.2
  101.8 685.1 %while.53 = (s32[]{:T(128)}, f32[2,2304,512]{2,1,0:T(8,128)}, f32[2,1,256,256]{3,2,1,0:T(8,128)}, f32[2,16]{1,0:T(2,128)S(1)}, s32[16]{0:T(128)S(1)}, /*index=5*...) while((s32[]{:T(128)}, f32[2,2304,512]{2,1,0:T(8,128)}, ...), condition=%wide.region_8.9_spmd.clone.clone, body=%wide.region_0.8_spmd.clone.clone.sunk | while | flops 12917768192 | bytes 100566328 | solution.py:127
  102.1 13.1 %while.54 = (s32[]{:T(128)}, f32[2,2304,512]{2,1,0:T(8,128)}, s32[4,3]{1,0:T(4,128)S(1)}, f32[4,2,256,256]{3,2,0,1:T(8,128)S(1)}, s32[]{:T(128)}) while((s32[]{:T(128)}, f32[2,2304,512]{2,1,0:T(8,128)}, s32[4,3]{1,0:T(4,128)S(1)}, f32[4,2,256,256]{3,2,0,1:T(8,128)S(1)}, s32[]{:T(128)}) %tuple.122), condition=%wide.while_cond.2, body=%wide.while_body.2.sunk | while | flops 2 | bytes 1048701 | solution.py:54
  143.4 47.6 %all-reduce.8.cloned.1.call-done = f32[4,256,256]{2,1,0:T(8,128)} async-done(((f32[4,256,256]{2,1,0:T(8,128)}), f32[4,256,256]{2,1,0:T(8,128)}) %all-reduce.8.cloned.1.call-update) | async-done | bytes 1048592 | tf_op jit(solution)/shard_map/while/body/eval_jaxpr/psum | solution.py:69
  218.6 52.2 %while.55 = (s32[]{:T(128)}, f32[2,2304,512]{2,1,0:T(8,128)}, s32[4]{0:T(128)S(1)}, s32[4]{0:T(128)S(1)}, f32[4,2,256,256]{3,2,0,1:T(8,128)S(1)}, /*index=5*/s32[]{:T(128)}, s32[]{:T(128)}, s32[]{:T(128)}, s32[]{:T(128)}) while((s32[]{:T(128)}, f32[2,2304,512]{2,1,0:T(8,128)}, s32[4]{0:T(128)S(1)}, s32[4]{0:T(128)S(1)}, ...), condition=%wide.region_3.3_spmd, body=%wide.region_2.2_spmd.sunk | while | flops 131080 | bytes 2621649 | solution.py:119
  272.5 13.1 %while.54 = (s32[]{:T(128)}, f32[2,2304,512]{2,1,0:T(8,128)}, s32[4,3]{1,0:T(4,128)S(1)}, f32[4,2,256,256]{3,2,0,1:T(8,128)S(1)}, s32[]{:T(128)}) while((s32[]{:T(128)}, f32[2,2304,512]{2,1,0:T(8,128)}, s32[4,3]{1,0:T(4,128)S(1)}, f32[4,2,256,256]{3,2,0,1:T(8,128)S(1)}, s32[]{:T(128)}) %tuple.122), condition=%wide.while_cond.2, body=%wide.while_body.2.sunk | while | flops 2 | bytes 1048701 | solution.py:54
  313.5 46.9 %all-reduce.8.cloned.1.call-done = f32[4,256,256]{2,1,0:T(8,128)} async-done(((f32[4,256,256]{2,1,0:T(8,128)}), f32[4,256,256]{2,1,0:T(8,128)}) %all-reduce.8.cloned.1.call-update) | async-done | bytes 1048592 | tf_op jit(solution)/shard_map/while/body/eval_jaxpr/psum | solution.py:69
  388.1 52.4 %while.55 = (s32[]{:T(128)}, f32[2,2304,512]{2,1,0:T(8,128)}, s32[4]{0:T(128)S(1)}, s32[4]{0:T(128)S(1)}, f32[4,2,256,256]{3,2,0,1:T(8,128)S(1)}, /*index=5*/s32[]{:T(128)}, s32[]{:T(128)}, s32[]{:T(128)}, s32[]{:T(128)}) while((s32[]{:T(128)}, f32[2,2304,512]{2,1,0:T(8,128)}, s32[4]{0:T(128)S(1)}, s32[4]{0:T(128)S(1)}, ...), condition=%wide.region_3.3_spmd, body=%wide.region_2.2_spmd.sunk | while | flops 131080 | bytes 2621649 | solution.py:119
  433.7 6.8 dynamic_update_slice.19
  443.2 13.1 %while.54 = (s32[]{:T(128)}, f32[2,2304,512]{2,1,0:T(8,128)}, s32[4,3]{1,0:T(4,128)S(1)}, f32[4,2,256,256]{3,2,0,1:T(8,128)S(1)}, s32[]{:T(128)}) while((s32[]{:T(128)}, f32[2,2304,512]{2,1,0:T(8,128)}, s32[4,3]{1,0:T(4,128)S(1)}, f32[4,2,256,256]{3,2,0,1:T(8,128)S(1)}, s32[]{:T(128)}) %tuple.122), condition=%wide.while_cond.2, body=%wide.while_body.2.sunk | while | flops 2 | bytes 1048701 | solution.py:54
  484.4 46.8 %all-reduce.8.cloned.1.call-done = f32[4,256,256]{2,1,0:T(8,128)} async-done(((f32[4,256,256]{2,1,0:T(8,128)}), f32[4,256,256]{2,1,0:T(8,128)}) %all-reduce.8.cloned.1.call-update) | async-done | bytes 1048592 | tf_op jit(solution)/shard_map/while/body/eval_jaxpr/psum | solution.py:69
  558.6 52.1 %while.55 = (s32[]{:T(128)}, f32[2,2304,512]{2,1,0:T(8,128)}, s32[4]{0:T(128)S(1)}, s32[4]{0:T(128)S(1)}, f32[4,2,256,256]{3,2,0,1:T(8,128)S(1)}, /*index=5*/s32[]{:T(128)}, s32[]{:T(128)}, s32[]{:T(128)}, s32[]{:T(128)}) while((s32[]{:T(128)}, f32[2,2304,512]{2,1,0:T(8,128)}, s32[4]{0:T(128)S(1)}, s32[4]{0:T(128)S(1)}, ...), condition=%wide.region_3.3_spmd, body=%wide.region_2.2_spmd.sunk | while | flops 131080 | bytes 2621649 | solution.py:119
  591.0 6.8 dynamic_update_slice.19
  613.7 13.1 %while.54 = (s32[]{:T(128)}, f32[2,2304,512]{2,1,0:T(8,128)}, s32[4,3]{1,0:T(4,128)S(1)}, f32[4,2,256,256]{3,2,0,1:T(8,128)S(1)}, s32[]{:T(128)}) while((s32[]{:T(128)}, f32[2,2304,512]{2,1,0:T(8,128)}, s32[4,3]{1,0:T(4,128)S(1)}, f32[4,2,256,256]{3,2,0,1:T(8,128)S(1)}, s32[]{:T(128)}) %tuple.122), condition=%wide.while_cond.2, body=%wide.while_body.2.sunk | while | flops 2 | bytes 1048701 | solution.py:54
  654.6 46.8 %all-reduce.8.cloned.1.call-done = f32[4,256,256]{2,1,0:T(8,128)} async-done(((f32[4,256,256]{2,1,0:T(8,128)}), f32[4,256,256]{2,1,0:T(8,128)}) %all-reduce.8.cloned.1.call-update) | async-done | bytes 1048592 | tf_op jit(solution)/shard_map/while/body/eval_jaxpr/psum | solution.py:69
  729.2 52.4 %while.55 = (s32[]{:T(128)}, f32[2,2304,512]{2,1,0:T(8,128)}, s32[4]{0:T(128)S(1)}, s32[4]{0:T(128)S(1)}, f32[4,2,256,256]{3,2,0,1:T(8,128)S(1)}, /*index=5*/s32[]{:T(128)}, s32[]{:T(128)}, s32[]{:T(128)}, s32[]{:T(128)}) while((s32[]{:T(128)}, f32[2,2304,512]{2,1,0:T(8,128)}, s32[4]{0:T(128)S(1)}, s32[4]{0:T(128)S(1)}, ...), condition=%wide.region_3.3_spmd, body=%wide.region_2.2_spmd.sunk | while | flops 131080 | bytes 2621649 | solution.py:119
  735.6 6.8 dynamic_update_slice.19
  793.9 19.3 %collective-permute-done.2 = f32[2,256,512]{2,1,0:T(8,128)S(1)} collective-permute-done((f32[2,256,512]{2,1,0:T(8,128)S(1)}, f32[2,256,512]{2,1,0:T(8,128)S(1)}, u32[]{:S(2)}, u32[]{:S(2)}) %collective-permute-start.2) | collective-permute-done | bytes 1048608 | tf_op jit(solution)/shard_map/ppermute | solution.py:14
  821.2 51.8 %collective-permute-done.3 = f32[2,2048,256]{2,1,0:T(8,128)} collective-permute-done((f32[2,2048,256]{2,1,0:T(8,128)}, f32[2,2048,256]{2,1,0:T(8,128)}, u32[]{:S(2)}, u32[]{:S(2)}) %collective-permute-start.3) | collective-permute-done | bytes 4194336 | tf_op jit(solution)/shard_map/ppermute | solution.py:14
  879.0 10.8 %psum.34 = f32[2,16]{1,0:T(2,128)} all-reduce(f32[2,16]{1,0:T(2,128)S(1)} %get-tuple-element.405), channel_id=1, replica_groups=mesh['row'=2,'col'=16,'mode'=4] {'mode'}, use_global_device_ids=true, to_apply=%region_11.12 | all-reduce | flops 32 | bytes 256 | tf_op jit(solution)/shard_map/psum | solution.py:132
  889.8 57.5 %all-reduce.6.cloned.1.call-done = f32[2,1,256,256]{3,2,1,0:T(8,128)} async-done(((f32[2,1,256,256]{3,2,1,0:T(8,128)}), f32[2,1,256,256]{3,2,1,0:T(8,128)}) %all-reduce.6.cloned.1.call-update) | async-done | bytes 524304 | tf_op jit(solution)/shard_map/psum | solution.py:133
  949.2 94.9 %all-reduce.4.cloned.1.call-done = f32[2,2048,256]{2,1,0:T(8,128)} async-done(((f32[2,2048,256]{2,1,0:T(8,128)}), f32[2,2048,256]{2,1,0:T(8,128)}) %all-reduce.4.cloned.1.call-update) | async-done | bytes 4194320 | tf_op jit(solution)/shard_map/psum | solution.py:132
  (287 shorter events, 456.5 us)
Async XLA Ops:
  8.0 50.0 %collective-permute-start = (f32[2,2048,256]{2,1,0:T(8,128)}, f32[2,2048,256]{2,1,0:T(8,128)S(1)}, u32[]{:S(2)}, u32[]{:S(2)}) collective-permute-start(f32[2,2048,256]{2,1,0:T(8,128)} %param.15), channel_id=1, source_target_pairs={{4,0},{8,4},{12,8},{16,12},{20,16},{24,20},{28,24},{32,28},{36,32}... | collective-permute-start | bytes 12582920 | tf_op jit(solution)/shard_map/ppermute | solution.py:14
  14.5 51.1 %copy-start.5 = (s32[32]{0:T(128)S(1)}, s32[32]{0:T(128)}, u32[]{:S(2)}) copy-start(s32[32]{0:T(128)} %param.18) | copy-start | bytes 388
  14.5 51.7 %copy-start.4 = (s32[2,16]{1,0:T(2,128)S(1)}, s32[2,16]{1,0:T(2,128)}, u32[]{:S(2)}) copy-start(s32[2,16]{1,0:T(2,128)} %param.19) | copy-start | bytes 388
  14.5 51.6 %copy-start.3 = (f32[2,1,256,256]{3,2,1,0:T(8,128)S(1)}, f32[2,1,256,256]{3,2,1,0:T(8,128)}, u32[]{:S(2)}) copy-start(f32[2,1,256,256]{3,2,1,0:T(8,128)} %param.16) | copy-start | bytes 1572868
  58.9 3.3 copy-start.2
  62.3 26.6 %collective-permute-start.1 = (f32[2,256,512]{2,1,0:T(8,128)S(1)}, f32[2,256,512]{2,1,0:T(8,128)S(1)}, u32[]{:S(2)}, u32[]{:S(2)}) collective-permute-start(f32[2,256,512]{2,1,0:T(8,128)S(1)} %slice.236), channel_id=1, source_target_pairs={{64,0},{65,1},{66,2},{67,3},{68,4},{69,5},{70,6},{71,7},{72,8},{73... | collective-permute-start | bytes 3145736 | tf_op jit(solution)/shard_map/ppermute | solution.py:14
  101.8 89.3 %all-reduce.8.cloned.1.call-start = ((), (), s32[]{:S(2)}) async-start(), calls=%async_computation.2 | async-start | bytes 2097152 | tf_op jit(solution)/shard_map/while/body/eval_jaxpr/psum | solution.py:69
  191.1 4.7 copy-start
  272.1 88.2 %all-reduce.8.cloned.1.call-start = ((), (), s32[]{:S(2)}) async-start(), calls=%async_computation.2 | async-start | bytes 2097152 | tf_op jit(solution)/shard_map/while/body/eval_jaxpr/psum | solution.py:69
  360.4 4.7 copy-start
  442.8 88.3 %all-reduce.8.cloned.1.call-start = ((), (), s32[]{:S(2)}) async-start(), calls=%async_computation.2 | async-start | bytes 2097152 | tf_op jit(solution)/shard_map/while/body/eval_jaxpr/psum | solution.py:69
  531.1 4.7 copy-start
  613.3 88.1 %all-reduce.8.cloned.1.call-start = ((), (), s32[]{:S(2)}) async-start(), calls=%async_computation.2 | async-start | bytes 2097152 | tf_op jit(solution)/shard_map/while/body/eval_jaxpr/psum | solution.py:69
  701.5 4.7 copy-start
  786.9 160.4 %all-reduce.6.cloned.1.call-start = ((), (), s32[]{:S(2)}) async-start(), calls=%async_computation.1 | async-start | bytes 1048576 | tf_op jit(solution)/shard_map/psum | solution.py:133
  788.3 24.9 %collective-permute-start.2 = (f32[2,256,512]{2,1,0:T(8,128)S(1)}, f32[2,256,512]{2,1,0:T(8,128)S(1)}, u32[]{:S(2)}, u32[]{:S(2)}) collective-permute-start(f32[2,256,512]{2,1,0:T(8,128)S(1)} %slice.178), channel_id=1, source_target_pairs={{0,64},{1,65},{2,66},{3,67},{4,68},{5,69},{6,70},{7,71},{8,72},{9,... | collective-permute-start | bytes 3145736 | tf_op jit(solution)/shard_map/ppermute | solution.py:14
  814.6 4.5 copy-start.1
  819.2 53.8 %collective-permute-start.3 = (f32[2,2048,256]{2,1,0:T(8,128)}, f32[2,2048,256]{2,1,0:T(8,128)}, u32[]{:S(2)}, u32[]{:S(2)}) collective-permute-start(f32[2,2048,256]{2,1,0:T(8,128)} %slice.238), channel_id=1, source_target_pairs={{0,4},{4,8},{8,12},{12,16},{16,20},{20,24},{24,28},{28,32},{32,36}... | collective-permute-start | bytes 12582920 | tf_op jit(solution)/shard_map/ppermute | solution.py:14
  821.1 223.0 %all-reduce.4.cloned.1.call-start = ((), (), s32[]{:S(2)}) async-start(), calls=%async_computation | async-start | bytes 8388608 | tf_op jit(solution)/shard_map/psum | solution.py:132
Sparse Core Ops, SparseCore 0:
  143.0 48.0 all-reduce.7
  313.0 47.3 all-reduce.7
  483.9 47.1 all-reduce.7
  654.2 47.2 all-reduce.7
Sparse Core Ops, SparseCore 1:
  821.2 126.1 all-reduce.5
  950.1 93.9 all-reduce.3
where the time goes:
time: 1070 us; the launch traced here: 1060 us
  waiting for transfers between devices  477 us (45%)
  local copies, waits for them, and re-layouts  206 us (19%)
  matrix products  202 us (19%)
  loops' own time  67.6 us (6%)
  other arithmetic  66.1 us (6%)
  between operations  15.5 us (1%)
  blocking collectives  10.8 us (1%)
    psum x4, waiting for transfers between devices, transform(): intensity = lax.psum(partial_int, 'mode')  188 us
    ppermute x4, waiting for transfers between devices, passed_along(): return lax.ppermute(x, axis, pairs)  136 us
    dynamic_update_slice x16, local copies, waits for them, and re-layouts, deposit(): lax.dynamic_update_slice(total, region + pieces[slot], (0, rows_blk[slot]...  106 us
    dot_general x32, matrix products, left_apply(): return jnp.einsum('kn,bmnj->bmkj', table, field, precision=HIGHEST)  104 us
    dot_general x32, matrix products, right_apply(): return jnp.einsum('bmkn,nj->bmkj', field, table, precision=HIGHEST)  98.2 us
    psum x1, waiting for transfers between devices, per_device(): grad_tile, shift_total = lax.psum((grad_tile, shift_grads), 'mode')  94.9 us
    another operation x4, loops' own time, advance(): grad_ext = lax.fori_loop(0, per_block, deposit, grad_ext)  62.3 us
    psum x1, waiting for transfers between devices, per_device(): probe_total = lax.psum(grad_probe, ('row', 'col')) / 16.0  57.5 us
  transfers between devices with their start and end apart: 10, of which 10 were waited for; matrix products, arithmetic and copies ran while one was open for 2% of the time, Pallas kernels for 0%

commit v1 on v0

v1 whole, which is shorter than its diff:
```python
import math
import functools
import numpy as np
import jax
import jax.numpy as jnp
from jax import lax
from jax.experimental import pallas as pl
from jax.experimental.pallas import tpu as pltpu
from jax.sharding import PartitionSpec as P

BF = jnp.bfloat16
F32 = jnp.float32


def hi_lo(x):
    hi = x.astype(BF)
    lo = (x - hi.astype(F32)).astype(BF)
    return hi, lo


def tables(window):
    half = window // 2
    n = np.arange(half)[:, None]
    j = np.arange(half)[None, :]
    scale = 1.0 / math.sqrt(window)
    forward, inverse = [], []
    for parity in range(2):
        angle = 2.0 * math.pi * ((n * (2 * j + parity)) % window) / window
        c, s = np.cos(angle) * scale, np.sin(angle) * scale
        forward.append(np.block([[c, -s], [s, c]]))
        inverse.append(np.block([[c.T, s.T], [-s.T, c.T]]))
    sides = []
    for axis in (1, 2):
        for table in (np.stack(forward), np.stack(inverse)):
            table = table.astype(np.float32)
            if axis == 2:
                table = np.swapaxes(table, 1, 2)
            hi = table.astype(BF)
            lo = (table - hi.astype(np.float32)).astype(BF)
            sides.append(np.concatenate([hi, lo, hi], axis=axis))
    order = np.concatenate([np.arange(0, window, 2), np.arange(1, window, 2)])
    shuffle = np.zeros((window, window), np.float32)
    shuffle[order, np.arange(window)] = 1.0
    return sides[0], sides[1], sides[2], sides[3], shuffle.astype(BF)


def cat(parts, axis):
    return jnp.concatenate(parts, axis=axis)


def mm(a, b):
    return jnp.dot(a, b, preferred_element_type=F32)


def make_compute(window, modes, slots, tile_rows, tile_cols):
    w, half = window, window // 2
    ch = 32
    ext_rows, ext_cols = tile_rows + w, tile_cols + w

    def kernel(meta, own, right, low, diag, probe, amps, rf, ri, lf, li, shuffle,
               g_own, g_right, g_low, g_diag, pg, along,
               ext, grad, amp_buf, win, fac, lhs, rhs, mid, far, near, amp_sem, sem):
        count = meta[2 * slots]
        mine = meta[2 * slots + 1]
        def quarters(whole, parts):
            pairs = []
            for k in range(4):
                for t in range(2):
                    down = slice(tile_rows, ext_rows) if k >= 2 else slice(0, tile_rows)
                    pairs.append((whole.at[2 * (k % 2) + t, :, down, :], parts[k].at[:, :, 128 * t:128 * t + 128]))
            return pairs

        loads = [
            pltpu.make_async_copy(part, inside, sem.at[k])
            for k, (inside, part) in enumerate(quarters(ext, (own, right, low, diag)))
        ]
        for copy in loads:
            copy.start()

        def amp_copies(slot, place):
            return [
                pltpu.make_async_copy(
                    amps.at[slot, :, 128 * t:128 * t + 128], amp_buf.at[place, t], amp_sem.at[place, t]
                )
                for t in range(2)
            ]

        for copy in amp_copies(0, 0):
            copy.start()

        def clear(i, carry):
            at = pl.multiple_of(i * ch, ch)
            for c in range(2):
                for t in range(4):
                    grad[t, c, pl.ds(at, ch), :] = jnp.zeros((ch, 128), F32)
            return carry

        lax.fori_loop(0, ext_rows // ch, clear, 0)
        pg[...] = jnp.zeros(pg.shape, F32)

        def no_shift(i, carry):
            along[0, i] = 0.0
            along[1, i] = 0.0
            return carry

        lax.fori_loop(0, slots, no_shift, 0)
        for copy in loads:
            copy.wait()

        def do_slot(slot, carry):
            row = meta[slot]
            col = meta[slots + slot]
            tile_at = col // 128
            off = lax.rem(col, 128)
            back = lax.rem(w + 128 - off, w + 128)
            place = lax.rem(slot, 2)
            for copy in amp_copies(slot, place):
                copy.wait()

            @pl.when(slot + 1 < count)
            def _():
                for copy in amp_copies(slot + 1, 1 - place):
                    copy.start()

            for c in range(2):
                for r in range(0, w, ch):
                    wide = cat([ext[tile_at + t, c, pl.ds(row + r, ch), :] for t in range(3)], 1)
                    win[c, r:r + ch, :] = pltpu.roll(wide, back, 1)[:, :w]

            for parity in range(2):
                a = cat([amp_buf[place, t, pl.ds(parity, half, stride=2), :] for t in range(2)], 1)
                a0, rest = a.astype(BF), None
                r1 = a - a0.astype(F32)
                a1 = r1.astype(BF)
                a2 = (r1 - a1.astype(F32)).astype(BF)
                fac[parity] = mm(a0, shuffle[...]) + mm(a1, shuffle[...]) + mm(a2, shuffle[...])

            for m in range(modes):
                for r in range(0, w, ch):
                    vre, vim = win[0, r:r + ch, :], win[1, r:r + ch, :]
                    pre, pim = probe[0, m, r:r + ch, :], probe[1, m, r:r + ch, :]
                    are = pre * vre - pim * vim
                    aim = pre * vim + pim * vre
                    for parity in range(2):
                        if parity == 0:
                            x = cat([are[:, :half] + are[:, half:], aim[:, :half] + aim[:, half:]], 1)
                        else:
                            x = cat([are[:, :half] - are[:, half:], aim[:, :half] - aim[:, half:]], 1)
                        hi, lo = hi_lo(x)
                        lhs[m, parity, r:r + ch, :w] = hi
                        lhs[m, parity, r:r + ch, w:] = lo
                for parity in range(2):
                    hi, lo = lhs[m, parity, :, :w], lhs[m, parity, :, w:]
                    mid[m, parity] = mm(cat([hi, hi, lo], 1), rf[parity])
                for r in range(0, half, ch):
                    e_top, e_bot = mid[m, 0, r:r + ch, :], mid[m, 0, half + r:half + r + ch, :]
                    o_top, o_bot = mid[m, 1, r:r + ch, :], mid[m, 1, half + r:half + r + ch, :]
                    for parity in range(2):
                        if parity == 0:
                            e, o = e_top + e_bot, o_top + o_bot
                        else:
                            e, o = e_top - e_bot, o_top - o_bot
                        hi, lo = hi_lo(cat([e[:, :half], o[:, :half]], 1))
                        rhs[m, parity, 0, r:r + ch, :] = hi
                        rhs[m, parity, 1, r:r + ch, :] = lo
                        hi, lo = hi_lo(cat([e[:, half:], o[:, half:]], 1))
                        rhs[m, parity, 0, half + r:half + r + ch, :] = hi
                        rhs[m, parity, 1, half + r:half + r + ch, :] = lo
                for parity in range(2):
                    hi, lo = rhs[m, parity, 0], rhs[m, parity, 1]
                    far[m, parity] = mm(lf[parity], cat([hi, hi, lo], 0))

            for parity in range(2):
                for r in range(0, half, ch):
                    total = None
                    for m in range(modes):
                        re = far[m, parity, r:r + ch, :]
                        im = far[m, parity, half + r:half + r + ch, :]
                        term = re * re + im * im
                        total = term if total is None else total + term
                    f = 0.25 * (1.0 - fac[parity, r:r + ch, :] * lax.rsqrt(total + 0.5))
                    fac[parity, r:r + ch, :] = f

            for m in range(modes):
                for parity in range(2):
                    for r in range(0, half, ch):
                        f = fac[parity, r:r + ch, :]
                        for part in range(2):
                            at = part * half + r
                            hi, lo = hi_lo(f * far[m, parity, at:at + ch, :])
                            rhs[m, parity, 0, at:at + ch, :] = hi
                            rhs[m, parity, 1, at:at + ch, :] = lo
                for parity in range(2):
                    hi, lo = rhs[m, parity, 0], rhs[m, parity, 1]
                    mid[m, parity] = mm(li[parity], cat([hi, hi, lo], 0))
                for r in range(0, half, ch):
                    e_re, e_im = mid[m, 0, r:r + ch, :], mid[m, 0, half + r:half + r + ch, :]
                    o_re, o_im = mid[m, 1, r:r + ch, :], mid[m, 1, half + r:half + r + ch, :]
                    for top in range(2):
                        if top == 0:
                            re, im = e_re + o_re, e_im + o_im
                        else:
                            re, im = e_re - o_re, e_im - o_im
                        at = top * half + r
                        for parity in range(2):
                            cols = slice(parity * half, parity * half + half)
                            hi, lo = hi_lo(cat([re[:, cols], im[:, cols]], 1))
                            lhs[m, parity, at:at + ch, :w] = hi
                            lhs[m, parity, at:at + ch, w:] = lo
                for parity in range(2):
                    hi, lo = lhs[m, parity, :, :w], lhs[m, parity, :, w:]
                    near[m, parity] = mm(cat([hi, hi, lo], 1), ri[parity])

            rows_sum = jnp.zeros((8, w), F32)
            cols_sum = jnp.zeros((8, w), F32)
            lanes = lax.broadcasted_iota(jnp.int32, (ch, w), 1)
            inner = (lanes >= 1) & (lanes <= w - 2)

            def near_of(m, r):
                e, o = near[m, 0, pl.ds(r, ch), :], near[m, 1, pl.ds(r, ch), :]
                s, d = e + o, e - o
                return cat([s[:, :half], d[:, :half]], 1), cat([s[:, half:], d[:, half:]], 1)

            for r in range(0, w, ch):
                gre = gim = None
                for m in range(modes):
                    nre, nim = near_of(m, r)
                    pre, pim = probe[0, m, r:r + ch, :], probe[1, m, r:r + ch, :]
                    tre = pre * nre + pim * nim
                    tim = pre * nim - pim * nre
                    gre = tre if gre is None else gre + tre
                    gim = tim if gim is None else gim + tim
                for c, g in ((0, gre), (1, gim)):
                    spread = pltpu.roll(cat([g, jnp.zeros((ch, 128), F32)], 1), off, 1)
                    for t in range(3):
                        grad[tile_at + t, c, pl.ds(row + r, ch), :] += spread[:, 128 * t:128 * t + 128]
                vre, vim = win[0, r:r + ch, :], win[1, r:r + ch, :]
                nre, nim = near_of(mine, r)
                pg[0, r:r + ch, :] += vre * nre + vim * nim
                pg[1, r:r + ch, :] += vre * nim - vim * nre
                dre = pltpu.roll(vre, w - 1, 1) - pltpu.roll(vre, 1, 1)
                dim = pltpu.roll(vim, w - 1, 1) - pltpu.roll(vim, 1, 1)
                t = jnp.where(inner, gre * dre + gim * dim, 0.0)
                cols_sum = cols_sum + jnp.sum(t.reshape(ch // 8, 8, w), axis=0)
                lo_r, hi_r = max(r, 1), min(r + ch, w - 1)
                up = [ext_rows_slice(win, c, r + 1, ch, w) for c in range(2)]
                dn = [ext_rows_slice(win, c, r - 1, ch, w) for c in range(2)]
                t = gre * (up[0] - dn[0]) + gim * (up[1] - dn[1])
                if lo_r != r or hi_r != r + ch:
                    idx = lax.broadcasted_iota(jnp.int32, (ch, w), 0) + r
                    t = jnp.where((idx >= lo_r) & (idx < hi_r), t, 0.0)
                rows_sum = rows_sum + jnp.sum(t.reshape(ch // 8, 8, w), axis=0)
            along[0, slot] = jnp.sum(rows_sum) * (0.5 / w)
            along[1, slot] = jnp.sum(cols_sum) * (0.5 / w)
            return carry

        def ext_rows_slice(ref, c, start, size, width):
            if start < 0:
                return cat([ref[c, 0:1, :], ref[c, 0:size - 1, :]], 0)
            if start + size > w:
                return cat([ref[c, start:w, :], ref[c, w - 1:w, :]], 0)
            return ref[c, start:start + size, :]

        lax.fori_loop(0, count, do_slot, 0)
        stores = [
            pltpu.make_async_copy(inside, part, sem.at[k])
            for k, (inside, part) in enumerate(quarters(grad, (g_own, g_right, g_low, g_diag)))
        ]
        for copy in stores:
            copy.start()
        for copy in stores:
            copy.wait()

    hbm = pl.BlockSpec(memory_space=pl.ANY)
    vmem = pl.BlockSpec(memory_space=pltpu.VMEM)
    smem = pl.BlockSpec(memory_space=pltpu.SMEM)
    shape = jax.ShapeDtypeStruct
    return pl.pallas_call(
        kernel,
        name="slots",
        in_specs=[smem, hbm, hbm, hbm, hbm, vmem, hbm, vmem, vmem, vmem, vmem, vmem],
        out_specs=[hbm, hbm, hbm, hbm, vmem, smem],
        out_shape=[
            shape((2, tile_rows, tile_cols), F32),
            shape((2, tile_rows, w), F32),
            shape((2, w, tile_cols), F32),
            shape((2, w, w), F32),
            shape((2, w, w), F32),
            shape((2, slots), F32),
        ],
        scratch_shapes=[
            pltpu.VMEM((ext_cols // 128, 2, ext_rows, 128), F32),
            pltpu.VMEM((ext_cols // 128, 2, ext_rows, 128), F32),
            pltpu.VMEM((2, 2, w, 128), F32),
            pltpu.VMEM((2, w, w), F32),
            pltpu.VMEM((2, half, w), F32),
            pltpu.VMEM((modes, 2, w, 2 * w), BF),
            pltpu.VMEM((modes, 2, 2, w, w), BF),
            pltpu.VMEM((modes, 2, w, w), F32),
            pltpu.VMEM((modes, 2, w, w), F32),
            pltpu.VMEM((modes, 2, w, w), F32),
            pltpu.SemaphoreType.DMA((2, 2)),
            pltpu.SemaphoreType.DMA((8,)),
        ],
        compiler_params=pltpu.CompilerParams(vmem_limit_bytes=60 << 20),
        cost_estimate=pl.CostEstimate(flops=10**11, bytes_accessed=10**7, transcendentals=0),
    )


def per_device(object_slab, probe_modes, amplitudes, scan_counts, scan_positions):
    window = probe_modes.shape[-1]
    tile_rows, tile_cols = object_slab.shape[1:]
    slots = amplitudes.shape[0]
    modes = lax.axis_size("mode")
    cols_n = lax.axis_size("col")
    rows_n = lax.axis_size("row")
    row_id, col_id, mode_id = lax.axis_index("row"), lax.axis_index("col"), lax.axis_index("mode")

    def diagonal(by):
        pairs = []
        for r in range(rows_n):
            for c in range(cols_n):
                if 0 <= r + by < rows_n and 0 <= c + by < cols_n:
                    pairs.append((r * cols_n + c, (r + by) * cols_n + c + by))
        return pairs

    def along(axis, by):
        n = lax.axis_size(axis)
        return [(i, i + by) for i in range(n) if 0 <= i + by < n]

    right = lax.ppermute(object_slab, "col", along("col", -1))
    top = object_slab[:, :window, :]
    low = lax.ppermute(top, "row", along("row", -1))
    diag = lax.ppermute(top, ("row", "col"), diagonal(-1))
    probe = lax.all_gather(probe_modes, "mode", axis=1, tiled=True)
    meta = jnp.concatenate([
        scan_positions[0] - row_id * tile_rows,
        scan_positions[1] - col_id * tile_cols,
        lax.dynamic_slice(scan_counts, (row_id * cols_n + col_id,), (1,)),
        mode_id[None].astype(jnp.int32),
    ])
    consts = [jnp.asarray(t) for t in tables(window)]
    compute = make_compute(window, modes, slots, tile_rows, tile_cols)
    g_own, g_right, g_low, g_diag, pg, shift = compute(
        meta, object_slab, right, low, diag, probe, amplitudes, *consts
    )
    from_left = lax.ppermute(g_right, "col", along("col", 1))
    from_up = lax.ppermute(g_low, "row", along("row", 1))
    from_diag = lax.ppermute(g_diag, ("row", "col"), diagonal(1))
    grad = g_own + from_left
    grad = grad.at[:, :window, :].add(from_up + from_diag)
    probe_total = lax.psum(pg, ("row", "col"))[:, None] / 16.0
    return (grad, probe_total, shift)


def solution(mesh):
    in_specs = (
        P(None, "row", "col"),
        P(None, "mode", None, None),
        P(("row", "col"), None, None),
        P(),
        P(None, ("row", "col")),
    )
    out_specs = (P(None, "row", "col"), P(None, "mode", None, None), P(None, ("row", "col")))
    return jax.shard_map(
        per_device, mesh=mesh, in_specs=in_specs, out_specs=out_specs, check_vma=False
    )
```

time: 1070 us -> 334 us (0.31); the launches traced: 1060 us -> 332 us
  waiting for transfers between devices: 477 us -> 224 us
  matrix products: 202 us -> 0 us
  local copies, waits for them, and re-layouts: 206 us -> 5.12 us
  Pallas kernels: 0 us -> 68 us
  loops' own time: 67.6 us -> 0 us
  other arithmetic: 66.1 us -> 8.1 us
  blocking collectives: 10.8 us -> 0 us
    dot_general x64 -> x0, matrix products: 202 us -> none  [the longest x32 104 us: left_apply(): return jnp.einsum('kn,bmnj->bmkj', table, field, precision=HIGHEST)]
    psum x6 -> x1, waiting for transfers between devices: 341 us -> 175 us  [per_device(): probe_total = lax.psum(pg, ('row', 'col'))[:, None] / 16.0]
    dynamic_update_slice x20 -> x0, local copies, waits for them, and re-layouts: 107 us -> none  [the longest x16 106 us: deposit(): lax.dynamic_update_slice(total, region + pieces[slot], (0, rows_blk[slot]...]
    ppermute x4 -> x6, waiting for transfers between devices: 136 us -> 49.5 us  [the longest x1 43.5 us: per_device(): diag = lax.ppermute(top, ('row', 'col'), diagonal(-1))]
    pallas_call x0 -> x1, Pallas kernels: none -> 68 us  [per_device(): compute(meta, object_slab, right, low, diag, probe, amplitudes, *consts)]
    another operation x9 -> x0, loops' own time: 67.6 us -> none  [the longest x4 62.3 us: advance(): grad_ext = lax.fori_loop(0, per_block, deposit, grad_ext)]
    gather x48 -> x0, local copies, waits for them, and re-layouts: 52.3 us -> none
    add x21 -> x1, other arithmetic: 34.6 us -> 4.01 us  [per_device(): grad = g_own + from_left]
  transfers between devices with their start and end apart: 10 -> 8, of which waited for: 10 -> 3; matrix products, arithmetic and copies ran while one was open for 2% -> 3% of each run, Pallas kernels for 0% -> 0%
where the time goes in v1:
time: 334 us; the launch traced here: 332 us
  waiting for transfers between devices  224 us (67%)
  Pallas kernels  68 us (20%)
  between operations  14.1 us (4%)
  starting transfers between devices  12.8 us (4%)
  other arithmetic  8.1 us (2%)
  local copies, waits for them, and re-layouts  5.12 us (2%)
    psum x1, waiting for transfers between devices, per_device(): probe_total = lax.psum(pg, ('row', 'col'))[:, None] / 16.0  175 us
    pallas_call x1, Pallas kernels, per_device(): compute(meta, object_slab, right, low, diag, probe, amplitudes, *consts)  68 us
    ppermute x1, waiting for transfers between devices, per_device(): diag = lax.ppermute(top, ('row', 'col'), diagonal(-1))  43.5 us
  transfers between devices with their start and end apart: 8, of which 3 were waited for; matrix products, arithmetic and copies ran while one was open for 3% of the time, Pallas kernels for 0%

profile of v1, /device:TPU:10, one launch (start us, length us, event | category | flops | bytes accessed | tf_op | source)
XLA Modules:
  0.0 332.2 jit_solution(11722963504075345927)
XLA Ops:
  7.2 0.0 all-gather.2.cloned.1.call-start
  7.2 3.6 %collective-permute-start = (f32[2,2048,256]{2,1,0:T(8,128)}, f32[2,2048,256]{2,1,0:T(8,128)}, u32[]{:S(2)}, u32[]{:S(2)}) collective-permute-start(f32[2,2048,256]{2,1,0:T(8,128)} %own.1), channel_id=1, source_target_pairs={{4,0},{8,4},{12,8},{16,12},{20,16},{24,20},{28,24},{32,28},{36,32}... | collective-permute-start | bytes 12582920 | tf_op jit(solution)/shard_map/ppermute | solution.py:331
  10.8 0.0 all-gather.2.cloned.1.call-update
  10.9 0.0 all-reduce.2.cloned.1.call-start
  10.9 1.1 slice.35
  12.0 1.9 collective-permute-start.2
  13.9 2.7 collective-permute-start.1
  16.6 1.2 dynamic_slice.3
  17.8 0.8 subtract_bitcast_fusion.1
  18.6 1.3 pad_add_fusion.meta
  19.9 43.5 %collective-permute-done.2.diag = f32[2,256,256]{2,1,0:T(8,128)S(1)} collective-permute-done((f32[2,256,256]{2,1,0:T(8,128)S(1)}, f32[2,256,256]{2,1,0:T(8,128)S(1)}, u32[]{:S(2)}, u32[]{:S(2)}) %collective-permute-start.2) | collective-permute-done | bytes 524320 | tf_op jit(solution)/shard_map/ppermute | solution.py:334
  63.4 5.9 %collective-permute-done.1.low = f32[2,256,256]{2,1,0:T(8,128)S(1)} collective-permute-done((f32[2,256,256]{2,1,0:T(8,128)S(1)}, f32[2,256,256]{2,1,0:T(8,128)S(1)}, u32[]{:S(2)}, u32[]{:S(2)}) %collective-permute-start.1) | collective-permute-done | bytes 524320 | tf_op jit(solution)/shard_map/ppermute | solution.py:333
  69.3 0.8 copy-done.2
  70.1 68.0 %slots.1 = (f32[2,2048,256]{2,1,0:T(8,128)}, f32[2,2048,256]{2,1,0:T(8,128)}, f32[2,256,256]{2,1,0:T(8,128)}, f32[2,256,256]{2,1,0:T(8,128)}, f32[2,256,256]{2,1,0:T(8,128)}, /*index=5*/f32[2,16]{1,0:T(2,128)}) custom-call(s32[34]{0:T(128)} %pad_add_fusion.meta, f32[2,2048,256]{2,1,0:T(8,128)} %own.1, f32[2,2048,256]{2,1,0:T(8,128)} %collective-permute-done.right, ...), custom_call_target="tpu_custom_call" | custom-call | flops 99999997952 | bytes 10000000 | tf_op jit(solution)/shard_map/slots/pallas_call | solution.py:344
  138.1 1.9 collective-permute-start.3
  140.0 1.3 collective-permute-start.4
  141.3 1.3 collective-permute-start.5
  142.6 0.0 all-reduce.2.cloned.1.call-update
  142.6 174.6 %all-reduce.2.cloned.1.call-done = f32[2,256,256]{2,1,0:T(8,128)} async-done(((f32[2,256,256]{2,1,0:T(8,128)}), f32[2,256,256]{2,1,0:T(8,128)}) %all-reduce.2.cloned.1.call-update) | async-done | bytes 524304 | tf_op jit(solution)/shard_map/psum | solution.py:352
  317.2 1.9 multiply_bitcast_fusion
  319.1 4.0 %add.23 = f32[2,2048,256]{2,1,0:T(8,128)S(1)} add(f32[2,2048,256]{2,1,0:T(8,128)} %get-tuple-element.21, f32[2,2048,256]{2,1,0:T(8,128)} %collective-permute-done.3) | non-fusion elementwise | flops 1048576 | bytes 12582912 | tf_op jit(solution)/shard_map/add | solution.py:350
  323.1 0.2 fusion
  323.3 0.0 copy-start
  323.3 2.0 copy-done
  (8 shorter events, 0.0 us)
Async XLA Ops:
  7.2 62.1 %all-gather.2.cloned.1.call-start = ((), (), s32[]{:S(2)}) async-start(), calls=%async_computation | async-start | bytes 2621440 | tf_op jit(solution)/shard_map/all_gather | solution.py:335
  7.2 62.1 %collective-permute-start = (f32[2,2048,256]{2,1,0:T(8,128)}, f32[2,2048,256]{2,1,0:T(8,128)}, u32[]{:S(2)}, u32[]{:S(2)}) collective-permute-start(f32[2,2048,256]{2,1,0:T(8,128)} %own.1), channel_id=1, source_target_pairs={{4,0},{8,4},{12,8},{16,12},{20,16},{24,20},{28,24},{32,28},{36,32}... | collective-permute-start | bytes 12582920 | tf_op jit(solution)/shard_map/ppermute | solution.py:331
  10.9 306.3 %all-reduce.2.cloned.1.call-start = ((), (), s32[]{:S(2)}) async-start(), calls=%async_computation.1 | async-start | bytes 1048576 | tf_op jit(solution)/shard_map/psum | solution.py:352
  12.0 51.4 %collective-permute-start.2 = (f32[2,256,256]{2,1,0:T(8,128)S(1)}, f32[2,256,256]{2,1,0:T(8,128)S(1)}, u32[]{:S(2)}, u32[]{:S(2)}) collective-permute-start(f32[2,256,256]{2,1,0:T(8,128)S(1)} %slice.35), channel_id=1, source_target_pairs={{68,0},{72,4},{76,8},{80,12},{84,16},{88,20},{92,24},{96,28},{100,... | collective-permute-start | bytes 1572872 | tf_op jit(solution)/shard_map/ppermute | solution.py:334
  13.9 55.4 %collective-permute-start.1 = (f32[2,256,256]{2,1,0:T(8,128)S(1)}, f32[2,256,256]{2,1,0:T(8,128)S(1)}, u32[]{:S(2)}, u32[]{:S(2)}) collective-permute-start(f32[2,256,256]{2,1,0:T(8,128)S(1)} %slice.35), channel_id=1, source_target_pairs={{64,0},{65,1},{66,2},{67,3},{68,4},{69,5},{70,6},{71,7},{72,8},{73... | collective-permute-start | bytes 1572872 | tf_op jit(solution)/shard_map/ppermute | solution.py:333
  63.4 5.9 %copy-start.1 = (f32[2,256,256]{2,1,0:T(8,128)}, f32[2,256,256]{2,1,0:T(8,128)S(1)}, u32[]{:S(2)}) copy-start(f32[2,256,256]{2,1,0:T(8,128)S(1)} %collective-permute-done.2.diag) | copy-start | bytes 1572868
  69.3 0.8 copy-start.2
  138.1 181.0 %collective-permute-start.3 = (f32[2,2048,256]{2,1,0:T(8,128)}, f32[2,2048,256]{2,1,0:T(8,128)}, u32[]{:S(2)}, u32[]{:S(2)}) collective-permute-start(f32[2,2048,256]{2,1,0:T(8,128)} %get-tuple-element.22), channel_id=1, source_target_pairs={{0,4},{4,8},{8,12},{12,16},{16,20},{20,24},{24,28},{28,32},{32,36}... | collective-permute-start | bytes 12582920 | tf_op jit(solution)/shard_map/ppermute | solution.py:347
  140.0 183.1 %collective-permute-start.4 = (f32[2,256,256]{2,1,0:T(8,128)}, f32[2,256,256]{2,1,0:T(8,128)S(1)}, u32[]{:S(2)}, u32[]{:S(2)}) collective-permute-start(f32[2,256,256]{2,1,0:T(8,128)} %get-tuple-element.23), channel_id=1, source_target_pairs={{0,64},{1,65},{2,66},{3,67},{4,68},{5,69},{6,70},{7,71},{8,72},{9,... | collective-permute-start | bytes 1572872 | tf_op jit(solution)/shard_map/ppermute | solution.py:348
  141.3 181.8 %collective-permute-start.5 = (f32[2,256,256]{2,1,0:T(8,128)}, f32[2,256,256]{2,1,0:T(8,128)S(1)}, u32[]{:S(2)}, u32[]{:S(2)}) collective-permute-start(f32[2,256,256]{2,1,0:T(8,128)} %get-tuple-element.24), channel_id=1, source_target_pairs={{0,68},{4,72},{8,76},{12,80},{16,84},{20,88},{24,92},{28,96},{32,1... | collective-permute-start | bytes 1572872 | tf_op jit(solution)/shard_map/ppermute | solution.py:349
  323.3 2.0 copy-start
Sparse Core Ops, SparseCore 0:
  11.0 33.3 all-gather.1
  142.8 174.3 all-reduce.1

commit v2 on v1

--- a/solution.py
+++ b/solution.py
@@ -307,32 +307,397 @@
     )
 
 
+MESH = pl.DeviceIdType.MESH
+
+
+def place():
+    return lax.axis_index("row"), lax.axis_index("col"), lax.axis_index("mode")
+
+
+def device(r, c, m):
+    return {"row": r, "col": c, "mode": m}
+
+
+def remote(src, dst, send, recv, to):
+    return pltpu.make_async_remote_copy(
+        src_ref=src, dst_ref=dst, send_sem=send, recv_sem=recv, device_id=to, device_id_type=MESH
+    )
+
+
+def greet(to):
+    pl.semaphore_signal(pltpu.get_barrier_semaphore(), inc=1, device_id=to, device_id_type=MESH)
+
+
+class Quarters:
+    def __init__(self, src, dst, modes, rows, to_col, sems):
+        r, c, m = place()
+        self.m, self.modes = m, modes
+        self.rows = rows // modes // CHUNKS
+        self.src, self.dst = src, dst
+        self.ys, self.yr, self.zs, self.zr, self.ts, self.tr = sems
+        self.peer = device(r, to_col, m)
+        self.next = device(r, c, lax.rem(m + 1, modes))
+        self.prev = device(r, c, lax.rem(m + modes - 1, modes))
+
+    def part(self, ref, owner, i):
+        at = pl.multiple_of((owner * CHUNKS + i) * self.rows, self.rows)
+        return ref.at[:, pl.ds(at, self.rows), :]
+
+    def first(self, i):
+        mine = self.part(self.src, self.m, i)
+        return remote(mine, self.part(self.dst, self.m, i), self.ys.at[i], self.yr.at[i], self.peer)
+
+    def ring(self, i, way):
+        mine = self.part(self.dst, self.m, i)
+        return remote(mine, mine, self.zs.at[way, i], self.zr.at[way, i], self.next if way == 0 else self.prev)
+
+    def relay(self, i):
+        back = self.modes - 1 if i < CHUNKS // 2 else 1
+        block = self.part(self.dst, lax.rem(self.m + back, self.modes), i)
+        return remote(block, block, self.ts.at[i], self.tr.at[i], self.next if i < CHUNKS // 2 else self.prev)
+
+    def start(self):
+        for i in range(CHUNKS):
+            self.first(i).start()
+
+    def sent(self):
+        for i in range(CHUNKS):
+            self.first(i).wait_send()
+
+    def take(self):
+        for i in range(CHUNKS):
+            self.first(i).wait_recv()
+            self.ring(i, 0).start()
+            self.ring(i, 1).start()
+
+    def finish(self):
+        for i in range(CHUNKS):
+            way = 0 if i < CHUNKS // 2 else 1
+            self.ring(i, way).wait_recv()
+            self.relay(i).start()
+        for i in range(CHUNKS):
+            way = 1 if i < CHUNKS // 2 else 0
+            self.ring(i, way).wait_recv()
+        for i in range(CHUNKS):
+            self.relay(i).wait_recv()
+        for i in range(CHUNKS):
+            self.ring(i, 0).wait_send()
+            self.ring(i, 1).wait_send()
+            self.relay(i).wait_send()
+
+
+CHUNKS = 4
+
+
+def quarter_sems():
+    one = pltpu.SemaphoreType.DMA((CHUNKS,))
+    two = pltpu.SemaphoreType.DMA((2, CHUNKS))
+    return [one, one, two, two, one, one]
+
+
+def make_spread(window, modes, tile_rows, tile_cols, rows_n, cols_n):
+    w = window
+
+    def kernel(tile, probe, right, low, diag, gathered, *sems):
+        quarter, (one_s, one_r, p_s, p_r, x_s, x_r, own_sem) = sems[:6], sems[6:]
+        r, c, m = place()
+        core = lax.rem(c, 2)
+        other = c + 1 - 2 * core
+        odd, even = core == 1, core == 0
+        has_left, has_right = c > 0, c < cols_n - 1
+        top = tile.at[:, pl.ds(0, w), :]
+
+        for k in range(1, modes):
+            greet(device(r, c, lax.rem(m + k, modes)))
+        greet(device(r, other, m))
+        greet(device(rows_n - 1 - r, c, m))
+        count = modes + 1
+        away = jnp.where(odd, jnp.minimum(c + 1, cols_n - 1), jnp.maximum(c - 1, 0))
+        has_away = jnp.where(odd, has_right, has_left)
+
+        @pl.when(has_away)
+        def _():
+            greet(device(r, away, m))
+
+        has_diag = has_away & jnp.where(odd, r == 0, r == 1)
+
+        @pl.when(has_diag)
+        def _():
+            greet(device(rows_n - 1 - r, away, m))
+
+        pl.semaphore_wait(
+            pltpu.get_barrier_semaphore(),
+            count + has_away.astype(jnp.int32) + has_diag.astype(jnp.int32),
+        )
+
+        strip = Quarters(tile, right, modes, tile_rows, away, quarter)
+        whole = remote(tile, right, one_s.at[0], one_r.at[0], device(r, other, m))
+        down = remote(top, low, one_s.at[1], one_r.at[1], device(rows_n - 1 - r, c, m))
+        corner = remote(top, diag, one_s.at[2], one_r.at[2], device(rows_n - 1 - r, away, m))
+        corner_on = remote(low, diag, one_s.at[2], one_r.at[2], device(r, other, m))
+
+        def probe_copy(k):
+            half = gathered.at[pl.ds(core, 1), pl.ds(m, 1)]
+            return remote(
+                probe.at[pl.ds(core, 1)], half, p_s.at[k], p_r.at[k], device(r, c, lax.rem(m + k, modes))
+            )
+
+        def probe_pass(k):
+            half = gathered.at[pl.ds(core, 1), pl.ds(lax.rem(m + modes - k, modes), 1)]
+            return remote(half, half, x_s.at[k], x_r.at[k], device(r, other, m))
+
+        @pl.when(even & has_left)
+        def _():
+            strip.start()
+
+        @pl.when(r == 1)
+        def _():
+            down.start()
+
+        @pl.when(even & has_diag)
+        def _():
+            corner.start()
+
+        for k in (1, 3, 2):
+            probe_copy(k).start()
+
+        @pl.when(odd)
+        def _():
+            whole.start()
+
+        keep = pltpu.make_async_copy(probe, gathered.at[:, pl.ds(m, 1)], own_sem)
+        keep.start()
+
+        @pl.when(odd & has_right)
+        def _():
+            strip.take()
+
+        @pl.when(r == 0)
+        def _():
+            down.wait_recv()
+
+        @pl.when(odd & (r == 0))
+        def _():
+            corner_on.start()
+
+        for k in (1, 3, 2):
+            probe_copy(k).wait_recv()
+            probe_pass(k).start()
+
+        @pl.when(odd & has_right)
+        def _():
+            strip.finish()
+
+        @pl.when(odd & has_diag)
+        def _():
+            corner.wait_recv()
+
+        @pl.when(even)
+        def _():
+            whole.wait_recv()
+
+        @pl.when(even & (r == 0))
+        def _():
+            corner_on.wait_recv()
+
+        for k in (1, 3, 2):
+            probe_pass(k).wait_recv()
+            probe_pass(k).wait_send()
+            probe_copy(k).wait_send()
+        keep.wait()
+
+        @pl.when(odd)
+        def _():
+            whole.wait_send()
+
+        @pl.when(odd & (r == 0))
+        def _():
+            corner_on.wait_send()
+
+        @pl.when(even & has_left)
+        def _():
+            strip.sent()
+
+        @pl.when(r == 1)
+        def _():
+            down.wait_send()
+
+        @pl.when(even & has_diag)
+        def _():
+            corner.wait_send()
+
+    hbm = pl.BlockSpec(memory_space=pl.ANY)
+    shape = jax.ShapeDtypeStruct
+    return pl.pallas_call(
+        kernel,
+        name="spread",
+        in_specs=[hbm, hbm],
+        out_specs=[hbm] * 4,
+        out_shape=[
+            shape((2, tile_rows, tile_cols), F32),
+            shape((2, w, tile_cols), F32),
+            shape((2, w, tile_cols), F32),
+            shape((2, modes, w, w), F32),
+        ],
+        scratch_shapes=quarter_sems() + [pltpu.SemaphoreType.DMA((3,))] * 2
+        + [pltpu.SemaphoreType.DMA((modes,))] * 4 + [pltpu.SemaphoreType.DMA],
+        compiler_params=pltpu.CompilerParams(collective_id=0, has_side_effects=True),
+    )
+
+
+def make_collect(window, modes, tile_rows, tile_cols, rows_n, cols_n):
+    w = window
+    group = rows_n * cols_n
+    piece = 2 * w // group
+
+    def kernel(g_right, g_low, g_diag, pg, right, low, diag, total, *sems):
+        quarter, (one_s, one_r, a_s, a_r, b_s, b_r, in_sem, got, mine) = sems[:6], sems[6:]
+        r, c, m = place()
+        me = r * cols_n + c
+        core = lax.rem(c, 2)
+        other = c + 1 - 2 * core
+        odd, even = core == 1, core == 0
+        away = jnp.where(odd, jnp.minimum(c + 1, cols_n - 1), jnp.maximum(c - 1, 0))
+        has_away = jnp.where(odd, c < cols_n - 1, c > 0)
+
+        def partner(k):
+            p = lax.rem(me + k, group)
+            return device(p // cols_n, lax.rem(p, cols_n), m)
+
+        def hello(k, carry):
+            greet(partner(k))
+            return carry
+
+        lax.fori_loop(1, group, hello, 0)
+        for k in (1, modes - 1):
+            greet(device(r, c, lax.rem(m + k, modes)))
+        pl.semaphore_wait(pltpu.get_barrier_semaphore(), group + 1)
+
+        strip = Quarters(g_right, right, modes, tile_rows, away, quarter)
+        whole = remote(g_right, right, one_s.at[0], one_r.at[0], device(r, other, m))
+        down = remote(g_low, low, one_s.at[1], one_r.at[1], device(rows_n - 1 - r, c, m))
+        to_c = jnp.minimum(c + 1, cols_n - 1)
+        corner = remote(g_diag, diag, one_s.at[2], one_r.at[2], device(rows_n - 1 - r, to_c, m))
+        send_diag = (r == 0) & (c < cols_n - 1)
+        take_diag = (r == 1) & (c > 0)
+
+        def scatter(k):
+            p = lax.rem(me + k, group)
+            rows = pl.ds(pl.multiple_of(p * piece, piece), piece)
+            return remote(pg.at[rows, :], got.at[k], a_s, a_r, partner(k))
+
+        def scatter_go(k, carry):
+            scatter(k).start()
+            return carry
+
+        lax.fori_loop(1, group, scatter_go, 0)
+        at_me = pl.ds(pl.multiple_of(me * piece, piece), piece)
+        own = pltpu.make_async_copy(pg.at[at_me, :], got.at[0], in_sem)
+        own.start()
+
+        @pl.when(odd & has_away)
+        def _():
+            strip.start()
+
+        @pl.when(r == 0)
+        def _():
+            down.start()
+
+        @pl.when(send_diag)
+        def _():
+            corner.start()
+
+        @pl.when(even)
+        def _():
+            whole.start()
+
+        own.wait()
+        rest = got.at[pl.ds(1, group - 1)]
+        pltpu.make_async_copy(rest, rest, a_r).wait()
+
+        def add(k, acc):
+            return acc + got[k]
+
+        mine[...] = lax.fori_loop(1, group, add, got[0]) * (1.0 / 16.0)
+
+        def share(k):
+            return remote(mine, total.at[at_me, :], b_s, b_r, partner(k))
+
+        def share_go(k, carry):
+            share(k).start()
+            return carry
+
+        keep = pltpu.make_async_copy(mine, total.at[at_me, :], in_sem)
+        keep.start()
+        lax.fori_loop(1, group, share_go, 0)
+
+        @pl.when(even & has_away)
+        def _():
+            strip.take()
+            strip.finish()
+
+        @pl.when(r == 1)
+        def _():
+            down.wait_recv()
+
+        @pl.when(take_diag)
+        def _():
+            corner.wait_recv()
+
+        @pl.when(odd)
+        def _():
+            whole.wait_recv()
+
+        keep.wait()
+        many = total.at[pl.ds(0, (group - 1) * piece), :]
+        pltpu.make_async_copy(many, many, b_r).wait()
+        pltpu.make_async_copy(rest, rest, a_s).wait()
+        pltpu.make_async_copy(many, many, b_s).wait()
+
+        @pl.when(odd & has_away)
+        def _():
+            strip.sent()
+
+        @pl.when(r == 0)
+        def _():
+            down.wait_send()
+
+        @pl.when(send_diag)
+        def _():
+            corner.wait_send()
+
+        @pl.when(even)
+        def _():
+            whole.wait_send()
+
+    hbm = pl.BlockSpec(memory_space=pl.ANY)
+    shape = jax.ShapeDtypeStruct
+    dma = pltpu.SemaphoreType.DMA
+    return pl.pallas_call(
+        kernel,
+        name="collect",
+        in_specs=[hbm] * 4,
+        out_specs=[hbm] * 4,
+        out_shape=[
+            shape((2, tile_rows, tile_cols), F32),
+            shape((2, w, tile_cols), F32),
+            shape((2, w, tile_cols), F32),
+            shape((2 * w, w), F32),
+        ],
+        scratch_shapes=quarter_sems() + [dma((3,))] * 2 + [dma] * 5
+        + [pltpu.VMEM((group, piece, w), F32), pltpu.VMEM((piece, w), F32)],
+        compiler_params=pltpu.CompilerParams(collective_id=1, has_side_effects=True),
+    )
+
+
 def per_device(object_slab, probe_modes, amplitudes, scan_counts, scan_positions):
     window = probe_modes.shape[-1]
     tile_rows, tile_cols = object_slab.shape[1:]
     slots = amplitudes.shape[0]
-    modes = lax.axis_size("mode")
-    cols_n = lax.axis_size("col")
-    rows_n = lax.axis_size("row")
-    row_id, col_id, mode_id = lax.axis_index("row"), lax.axis_index("col"), lax.axis_index("mode")
-
-    def diagonal(by):
-        pairs = []
-        for r in range(rows_n):
-            for c in range(cols_n):
-                if 0 <= r + by < rows_n and 0 <= c + by < cols_n:
-                    pairs.append((r * cols_n + c, (r + by) * cols_n + c + by))
-        return pairs
-
-    def along(axis, by):
-        n = lax.axis_size(axis)
-        return [(i, i + by) for i in range(n) if 0 <= i + by < n]
-
-    right = lax.ppermute(object_slab, "col", along("col", -1))
-    top = object_slab[:, :window, :]
-    low = lax.ppermute(top, "row", along("row", -1))
-    diag = lax.ppermute(top, ("row", "col"), diagonal(-1))
-    probe = lax.all_gather(probe_modes, "mode", axis=1, tiled=True)
+    modes, cols_n, rows_n = (lax.axis_size(a) for a in ("mode", "col", "row"))
+    row_id, col_id, mode_id = place()
+    sizes = (window, modes, tile_rows, tile_cols, rows_n, cols_n)
+    right, low, diag, probe = make_spread(*sizes)(object_slab, probe_modes)
     meta = jnp.concatenate([
         scan_positions[0] - row_id * tile_rows,
         scan_positions[1] - col_id * tile_cols,
@@ -344,13 +709,15 @@
     g_own, g_right, g_low, g_diag, pg, shift = compute(
         meta, object_slab, right, low, diag, probe, amplitudes, *consts
     )
-    from_left = lax.ppermute(g_right, "col", along("col", 1))
-    from_up = lax.ppermute(g_low, "row", along("row", 1))
-    from_diag = lax.ppermute(g_diag, ("row", "col"), diagonal(1))
-    grad = g_own + from_left
-    grad = grad.at[:, :window, :].add(from_up + from_diag)
-    probe_total = lax.psum(pg, ("row", "col"))[:, None] / 16.0
-    return (grad, probe_total, shift)
+    from_left, from_up, from_diag, total = make_collect(*sizes)(
+        g_right, g_low, g_diag, pg.reshape(2 * window, window)
+    )
+    below, inner = row_id > 0, col_id > 0
+    strip = jnp.where(inner, from_left, 0.0)
+    top = jnp.where(below, from_up, 0.0) + jnp.where(below & inner, from_diag, 0.0)
+    top = jnp.pad(top, ((0, 0), (0, tile_rows - window), (0, 0)))
+    grad = g_own + strip + top
+    return (grad, total.reshape(2, 1, window, window), shift)
 
 
 def solution(mesh):

time: 334 us -> 195 us (0.58)
  waiting for transfers between devices: 224 us -> 0 us
  Pallas kernels: 68 us -> 180 us
  between operations: 14.1 us -> 0.69 us
  starting transfers between devices: 12.8 us -> 0 us
    psum x1 -> x0, waiting for transfers between devices: 175 us -> none  [per_device(): probe_total = lax.psum(pg, ('row', 'col'))[:, None] / 16.0]
    pallas_call x0 -> x2, Pallas kernels: none -> 77.3 us  [the longest x1 50 us: per_device(): make_collect(*sizes)(g_right, g_low, g_diag, pg.reshape(2 * window, window))]
    ppermute x6 -> x0, waiting for transfers between devices: 49.5 us -> none  [the longest x1 43.5 us: per_device(): diag = lax.ppermute(top, ('row', 'col'), diagonal(-1))]
    pallas_call x1, Pallas kernels: 68 us -> 102 us  [per_device(): compute(meta, object_slab, right, low, diag, probe, amplitudes, *consts)]
    ppermute x6 -> x0, starting transfers between devices: 12.7 us -> none  [the longest x1 3.62 us: per_device(): right = lax.ppermute(object_slab, 'col', along('col', -1))]
    add x1 -> x2, other arithmetic: 4.01 us -> 7.38 us  [the longest x1 6.1 us: per_device(): grad = g_own + strip + top]
  transfers between devices with their start and end apart: 8 -> 0, of which waited for: 3 -> 0; matrix products, arithmetic and copies ran while one was open for 3% -> 0% of each run, Pallas kernels for 0% -> 0%
where the time goes in v2:
time: 195 us; the launch traced here: 192 us
  Pallas kernels  180 us (92%)
  other arithmetic  9.38 us (5%)
  local copies, waits for them, and re-layouts  2.04 us (1%)
    pallas_call x1, Pallas kernels, per_device(): compute(meta, object_slab, right, low, diag, probe, amplitudes, *consts)  102 us
    pallas_call x1, Pallas kernels, per_device(): make_collect(*sizes)(g_right, g_low, g_diag, pg.reshape(2 * window, window))  50 us
    pallas_call x1, Pallas kernels, per_device(): right, low, diag, probe = make_spread(*sizes)(object_slab, probe_modes)  27.3 us
    add x1, other arithmetic, per_device(): grad = g_own + strip + top  6.1 us

profile of v2, /device:TPU:10, one launch (start us, length us, event | category | flops | bytes accessed | tf_op | source)
XLA Modules:
  0.0 191.8 jit_solution(2834509677661365286)
XLA Ops:
  0.6 1.2 dynamic_slice.3
  1.9 0.8 subtract_bitcast_fusion.1
  2.6 1.2 pad_add_fusion.1.meta
  3.9 27.3 %spread.1 = (f32[2,2048,256]{2,1,0:T(8,128)}, f32[2,256,256]{2,1,0:T(8,128)}, f32[2,256,256]{2,1,0:T(8,128)}, f32[2,4,256,256]{3,2,1,0:T(8,128)}) custom-call(f32[2,2048,256]{2,1,0:T(8,128)} %own.1, f32[2,1,256,256]{3,2,1,0:T(8,128)} %probe.1), custom_call_target="tpu_custom_call" | custom-call | tf_op jit(solution)/shard_map/spread/pallas_call | solution.py:700
  31.2 102.4 %slots.1 = (f32[2,2048,256]{2,1,0:T(8,128)}, f32[2,2048,256]{2,1,0:T(8,128)}, f32[2,256,256]{2,1,0:T(8,128)}, f32[2,256,256]{2,1,0:T(8,128)}, f32[2,256,256]{2,1,0:T(8,128)}, /*index=5*/f32[2,16]{1,0:T(2,128)}) custom-call(s32[34]{0:T(128)} %pad_add_fusion.1.meta, f32[2,2048,256]{2,1,0:T(8,128)} %own.1, f32[2,2048,256]{2,1,0:T(8,128)} %get-tuple-element.17.right, ...), custom_call_target="tpu_custom_call" | custom-call | flops 99999997952 | bytes 10000000 | tf_op jit(solution)/shard_map/slots/pallas_call | solution.py:709
  133.6 50.0 %collect.1 = (f32[2,2048,256]{2,1,0:T(8,128)}, f32[2,256,256]{2,1,0:T(8,128)}, f32[2,256,256]{2,1,0:T(8,128)}, f32[512,256]{1,0:T(8,128)}) custom-call(f32[2,2048,256]{2,1,0:T(8,128)} %get-tuple-element.22.g_right, f32[2,256,256]{2,1,0:T(8,128)} %get-tuple-element.23.g_low, f32[2,256,256]{2,1,0:T(8,128)} %get-tuple-element.24.g_diag, f32[512,256]{1,0:T(8,128)} %bitcast.10), custom_call_target="tpu_custom_call" | custom-call | tf_op jit(solution)/shard_map/collect/pallas_call | solution.py:712
  183.6 1.3 select_add_fusion
  184.9 0.0 copy-start
  184.9 6.1 %pad_add_fusion = f32[2,2048,256]{2,1,0:T(8,128)} fusion(f32[2,256,256]{2,1,0:T(8,128)S(1)} %select_add_fusion, f32[2,2048,256]{2,1,0:T(8,128)} %get-tuple-element.21, f32[2,2048,256]{2,1,0:T(8,128)} %get-tuple-element.26, pred[]{:T(512)S(6)} %gt.6), kind=kLoop, calls=%fused_computation | loop fusion | flops 3145728 | bytes 13107201 | tf_op jit(solution)/shard_map/add | solution.py:719
  191.0 0.0 copy-done
  191.0 0.8 copy.15
Async XLA Ops:
  184.9 6.1 %copy-start = (f32[512,256]{1,0:T(8,128)S(1)}, f32[512,256]{1,0:T(8,128)}, u32[]{:S(2)}) copy-start(f32[512,256]{1,0:T(8,128)} %get-tuple-element.29) | copy-start | bytes 1572868

commit v3 on v1

--- a/solution.py
+++ b/solution.py
@@ -52,16 +52,16 @@
     return jnp.dot(a, b, preferred_element_type=F32)
 
 
-def make_compute(window, modes, slots, tile_rows, tile_cols):
+def make_compute(window, modes, slots, tile_rows, tile_cols, cols_n):
     w, half = window, window // 2
     ch = 32
     ext_rows, ext_cols = tile_rows + w, tile_cols + w
 
-    def kernel(meta, own, right, low, diag, probe, amps, rf, ri, lf, li, shuffle,
+    def kernel(positions, counts, own, right, low, diag, probe, amps, rf, ri, lf, li, shuffle,
                g_own, g_right, g_low, g_diag, pg, along,
                ext, grad, amp_buf, win, fac, lhs, rhs, mid, far, near, amp_sem, sem):
-        count = meta[2 * slots]
-        mine = meta[2 * slots + 1]
+        row_id, col_id, mine = place()
+        count = counts[row_id * cols_n + col_id]
         def quarters(whole, parts):
             pairs = []
             for k in range(4):
@@ -108,8 +108,8 @@
             copy.wait()
 
         def do_slot(slot, carry):
-            row = meta[slot]
-            col = meta[slots + slot]
+            row = positions[0, slot] - row_id * tile_rows
+            col = positions[1, slot] - col_id * tile_cols
             tile_at = col // 128
             off = lax.rem(col, 128)
             back = lax.rem(w + 128 - off, w + 128)
@@ -278,7 +278,7 @@
     return pl.pallas_call(
         kernel,
         name="slots",
-        in_specs=[smem, hbm, hbm, hbm, hbm, vmem, hbm, vmem, vmem, vmem, vmem, vmem],
+        in_specs=[smem, smem, hbm, hbm, hbm, hbm, vmem, hbm, vmem, vmem, vmem, vmem, vmem],
         out_specs=[hbm, hbm, hbm, hbm, vmem, smem],
         out_shape=[
             shape((2, tile_rows, tile_cols), F32),
@@ -307,50 +307,387 @@
     )
 
 
+MESH = pl.DeviceIdType.MESH
+
+
+def place():
+    return lax.axis_index("row"), lax.axis_index("col"), lax.axis_index("mode")
+
+
+def device(r, c, m):
+    return {"row": r, "col": c, "mode": m}
+
+
+def remote(src, dst, send, recv, to):
+    return pltpu.make_async_remote_copy(
+        src_ref=src, dst_ref=dst, send_sem=send, recv_sem=recv, device_id=to, device_id_type=MESH
+    )
+
+
+def greet(to):
+    pl.semaphore_signal(pltpu.get_barrier_semaphore(), inc=1, device_id=to, device_id_type=MESH)
+
+
+class Quarters:
+    def __init__(self, src, dst, modes, rows, r, c, chunks, sems):
+        me_r, me_c, m = place()
+        self.m, self.modes, self.chunks = m, modes, chunks
+        self.rows = rows // modes // chunks
+        self.src, self.dst = src, dst
+        self.ys, self.yr, self.zs, self.zr, self.ts, self.tr = sems
+        self.peer = device(r, c, m)
+        self.next = device(me_r, me_c, lax.rem(m + 1, modes))
+        self.prev = device(me_r, me_c, lax.rem(m + modes - 1, modes))
+
+    def part(self, ref, owner, i):
+        at = pl.multiple_of((owner * self.chunks + i) * self.rows, self.rows)
+        return ref.at[:, pl.ds(at, self.rows), :]
+
+    def first(self, i):
+        mine = self.part(self.src, self.m, i)
+        return remote(mine, self.part(self.dst, self.m, i), self.ys.at[i], self.yr.at[i], self.peer)
+
+    def ring(self, i, way):
+        mine = self.part(self.dst, self.m, i)
+        return remote(mine, mine, self.zs.at[way, i], self.zr.at[way, i], self.next if way == 0 else self.prev)
+
+    def way(self, i):
+        return 0 if i < self.chunks // 2 else 1
+
+    def relay(self, i):
+        back = self.modes - 1 if self.way(i) == 0 else 1
+        block = self.part(self.dst, lax.rem(self.m + back, self.modes), i)
+        return remote(block, block, self.ts.at[i], self.tr.at[i], self.next if self.way(i) == 0 else self.prev)
+
+    def start(self):
+        for i in range(self.chunks):
+            self.first(i).start()
+
+    def sent(self):
+        for i in range(self.chunks):
+            self.first(i).wait_send()
+
+    def take(self, some=None):
+        for i in range(self.chunks) if some is None else some:
+            self.first(i).wait_recv()
+            self.ring(i, 0).start()
+            self.ring(i, 1).start()
+
+    def turn(self):
+        for i in range(self.chunks):
+            self.ring(i, self.way(i)).wait_recv()
+            self.relay(i).start()
+
+    def finish(self):
+        for i in range(self.chunks):
+            self.ring(i, 1 - self.way(i)).wait_recv()
+            self.relay(i).wait_recv()
+        for i in range(self.chunks):
+            self.ring(i, 0).wait_send()
+            self.ring(i, 1).wait_send()
+            self.relay(i).wait_send()
+
+
+STRIP, EDGE = 4, 2
+
+
+def quarter_sems(chunks):
+    one = pltpu.SemaphoreType.DMA((chunks,))
+    two = pltpu.SemaphoreType.DMA((2, chunks))
+    return [one, one, two, two, one, one]
+
+
+def when(cond, *steps):
+    @pl.when(cond)
+    def _():
+        for step in steps:
+            step()
+
+
+def make_spread(window, modes, tile_rows, tile_cols, rows_n, cols_n):
+    w = window
+
+    def kernel(tile, probe, right, low, diag, gathered, *sems):
+        strip_sems, low_sems, diag_sems = sems[:6], sems[6:12], sems[12:18]
+        one_s, one_r, p_s, p_r, x_s, x_r, own_sem = sems[18:]
+        r, c, m = place()
+        core = lax.rem(c, 2)
+        other = c + 1 - 2 * core
+        odd, even = core == 1, core == 0
+        away = jnp.where(odd, jnp.minimum(c + 1, cols_n - 1), jnp.maximum(c - 1, 0))
+        has_away = jnp.where(odd, c < cols_n - 1, c > 0)
+        has_diag = has_away & jnp.where(odd, r == 0, r == 1)
+        flip = rows_n - 1 - r
+
+        for k in range(1, modes):
+            greet(device(r, c, lax.rem(m + k, modes)))
+        greet(device(r, other, m))
+        greet(device(flip, c, m))
+        when(has_away, lambda: greet(device(r, away, m)))
+        when(has_diag, lambda: greet(device(flip, away, m)))
+        pl.semaphore_wait(
+            pltpu.get_barrier_semaphore(),
+            modes + 1 + has_away.astype(jnp.int32) + has_diag.astype(jnp.int32),
+        )
+
+        strip = Quarters(tile, right, modes, tile_rows, r, away, STRIP, strip_sems)
+        down = Quarters(tile, low, modes, w, flip, c, EDGE, low_sems)
+        corner = Quarters(tile, diag, modes, w, flip, away, EDGE, diag_sems)
+        whole = remote(tile, right, one_s.at[0], one_r.at[0], device(r, other, m))
+        corner_on = remote(low, diag, one_s.at[1], one_r.at[1], device(r, other, m))
+
+        def probe_copy(k):
+            half = gathered.at[pl.ds(core, 1), pl.ds(m, 1)]
+            return remote(
+                probe.at[pl.ds(core, 1)], half, p_s.at[k], p_r.at[k], device(r, c, lax.rem(m + k, modes))
+            )
+
+        def probe_pass(k):
+            half = gathered.at[pl.ds(core, 1), pl.ds(lax.rem(m + modes - k, modes), 1)]
+            return remote(half, half, x_s.at[k], x_r.at[k], device(r, other, m))
+
+        far = (1, modes - 1, 2)
+        when(even & has_away, strip.start)
+        when(r == 1, down.start)
+        when(even & has_diag, corner.start)
+        for k in far:
+            probe_copy(k).start()
+        when(odd, whole.start)
+        keep = pltpu.make_async_copy(probe, gathered.at[:, pl.ds(m, 1)], own_sem)
+        keep.start()
+
+        when(odd & has_away, lambda: strip.take([0]))
+        when(r == 0, down.take)
+        when(odd & has_diag, corner.take)
+        when(odd & has_away, lambda: strip.take([1, 2, 3]))
+        when(r == 0, down.turn)
+        when(odd & has_diag, corner.turn)
+        when(odd & has_away, strip.turn)
+        when(r == 0, down.finish)
+        when(odd & (r == 0), corner_on.start)
+        for k in far:
+            probe_copy(k).wait_recv()
+            probe_pass(k).start()
+        when(odd & has_diag, corner.finish)
+        when(odd & has_away, strip.finish)
+        when(even, whole.wait_recv)
+        when(even & (r == 0), corner_on.wait_recv)
+        for k in far:
+            probe_pass(k).wait_recv()
+            probe_pass(k).wait_send()
+            probe_copy(k).wait_send()
+        keep.wait()
+        when(odd, whole.wait_send)
+        when(odd & (r == 0), corner_on.wait_send)
+        when(even & has_away, strip.sent)
+        when(r == 1, down.sent)
+        when(even & has_diag, corner.sent)
+
+    hbm = pl.BlockSpec(memory_space=pl.ANY)
+    shape = jax.ShapeDtypeStruct
+    dma = pltpu.SemaphoreType.DMA
+    return pl.pallas_call(
+        kernel,
+        name="spread",
+        in_specs=[hbm, hbm],
+        out_specs=[hbm] * 4,
+        out_shape=[
+            shape((2, tile_rows, tile_cols), F32),
+            shape((2, w, tile_cols), F32),
+            shape((2, w, tile_cols), F32),
+            shape((2, modes, w, w), F32),
+        ],
+        scratch_shapes=quarter_sems(STRIP) + quarter_sems(EDGE) + quarter_sems(EDGE)
+        + [dma((2,))] * 2 + [dma((modes,))] * 4 + [dma],
+        compiler_params=pltpu.CompilerParams(collective_id=0, has_side_effects=True),
+    )
+
+
+def make_collect(window, modes, tile_rows, tile_cols, rows_n, cols_n):
+    w = window
+    chips = rows_n * cols_n // 2
+    piece = w // chips
+
+    def kernel(g_right, g_low, g_diag, pg, right, low, diag, total, *sems):
+        strip_sems, low_sems, diag_sems = sems[:6], sems[6:12], sems[12:18]
+        one_s, one_r, x_s, x_r, y_s, y_r, a_s, a_r, b_s, b_r, in_sem, pair, got, mine = sems[18:]
+        r, c, m = place()
+        core = lax.rem(c, 2)
+        chip = r * (cols_n // 2) + c // 2
+        other = c + 1 - 2 * core
+        odd, even = core == 1, core == 0
+        away = jnp.where(odd, jnp.minimum(c + 1, cols_n - 1), jnp.maximum(c - 1, 0))
+        has_away = jnp.where(odd, c < cols_n - 1, c > 0)
+        flip = rows_n - 1 - r
+        over = jnp.where(r == 0, jnp.minimum(c + 1, cols_n - 1), jnp.maximum(c - 1, 0))
+        has_over = jnp.where(r == 0, c < cols_n - 1, c > 0)
+
+        def partner(k):
+            p = lax.rem(chip + k, chips)
+            return device(p // (cols_n // 2), 2 * lax.rem(p, cols_n // 2) + core, m)
+
+        def hello(k, carry):
+            greet(partner(k))
+            return carry
+
+        lax.fori_loop(1, chips, hello, 0)
+        greet(device(r, other, m))
+        for k in (1, modes - 1):
+            greet(device(r, c, lax.rem(m + k, modes)))
+        when(has_away, lambda: greet(device(r, away, m)))
+        when(has_over, lambda: greet(device(flip, over, m)))
+        pl.semaphore_wait(
+            pltpu.get_barrier_semaphore(),
+            chips + 2 + has_away.astype(jnp.int32) + has_over.astype(jnp.int32),
+        )
+
+        strip = Quarters(g_right, right, modes, tile_rows, r, away, STRIP, strip_sems)
+        down = Quarters(g_low, low, modes, w, flip, c, EDGE, low_sems)
+        corner = Quarters(g_diag, diag, modes, w, flip, over, EDGE, diag_sems)
+        whole = remote(g_right, right, one_s, one_r, device(r, other, m))
+        my_half = pl.ds(pl.multiple_of(core * w, w), w)
+        its_half = pl.ds(pl.multiple_of((1 - core) * w, w), w)
+
+        swap = remote(pg.at[its_half, :], pair.at[0], x_s, x_r, device(r, other, m))
+        swap.start()
+        own = pltpu.make_async_copy(pg.at[my_half, :], pair.at[1], in_sem)
+        own.start()
+        when(odd & has_away, strip.start)
+        when(r == 0, down.start)
+        when((r == 0) & has_over, corner.start)
+
+        own.wait()
+        swap.wait_recv()
+        pair[1] = pair[0] + pair[1]
+        when(even, whole.start)
+
+        def scatter(k):
+            p = lax.rem(chip + k, chips)
+            rows = pl.ds(pl.multiple_of(p * piece, piece), piece)
+            return remote(pair.at[1, rows, :], got.at[k], a_s, a_r, partner(k))
+
+        def scatter_go(k, carry):
+            scatter(k).start()
+            return carry
+
+        lax.fori_loop(1, chips, scatter_go, 0)
+        when(even & has_away, lambda: strip.take([0]))
+        when(r == 1, down.take)
+        when((r == 1) & has_over, corner.take)
+
+        rest = got.at[pl.ds(1, chips - 1)]
+        pltpu.make_async_copy(rest, rest, a_r).wait()
+        at_chip = pl.ds(pl.multiple_of(chip * piece, piece), piece)
+
+        def add(k, acc):
+            return acc + got[k]
+
+        mine[...] = lax.fori_loop(1, chips, add, pair[1, at_chip, :]) * (1.0 / 16.0)
+        at_me = pl.ds(pl.multiple_of(core * w + chip * piece, piece), piece)
+
+        def share(k):
+            return remote(mine, total.at[at_me, :], b_s, b_r, partner(k))
+
+        def share_go(k, carry):
+            share(k).start()
+            return carry
+
+        keep = pltpu.make_async_copy(mine, total.at[at_me, :], in_sem)
+        keep.start()
+        lax.fori_loop(1, chips, share_go, 0)
+
+        when(even & has_away, lambda: strip.take([1, 2, 3]))
+        when(r == 1, down.turn)
+        when((r == 1) & has_over, corner.turn)
+        when(even & has_away, strip.turn)
+
+        keep.wait()
+        many = total.at[pl.ds(0, (chips - 1) * piece), :]
+        pltpu.make_async_copy(many, many, b_r).wait()
+        give = remote(total.at[my_half, :], total.at[my_half, :], y_s, y_r, device(r, other, m))
+        give.start()
+
+        when(r == 1, down.finish)
+        when((r == 1) & has_over, corner.finish)
+        when(even & has_away, strip.finish)
+        when(odd, whole.wait_recv)
+        give.wait_recv()
+        give.wait_send()
+        swap.wait_send()
+        pltpu.make_async_copy(rest, rest, a_s).wait()
+        pltpu.make_async_copy(many, many, b_s).wait()
+        when(odd & has_away, strip.sent)
+        when(r == 0, down.sent)
+        when((r == 0) & has_over, corner.sent)
+        when(even, whole.wait_send)
+
+    hbm = pl.BlockSpec(memory_space=pl.ANY)
+    shape = jax.ShapeDtypeStruct
+    dma = pltpu.SemaphoreType.DMA
+    return pl.pallas_call(
+        kernel,
+        name="collect",
+        in_specs=[hbm] * 4,
+        out_specs=[hbm] * 4,
+        out_shape=[
+            shape((2, tile_rows, tile_cols), F32),
+            shape((2, w, tile_cols), F32),
+            shape((2, w, tile_cols), F32),
+            shape((2 * w, w), F32),
+        ],
+        scratch_shapes=quarter_sems(STRIP) + quarter_sems(EDGE) + quarter_sems(EDGE) + [dma] * 11
+        + [pltpu.VMEM((2, w, w), F32), pltpu.VMEM((chips, piece, w), F32), pltpu.VMEM((piece, w), F32)],
+        compiler_params=pltpu.CompilerParams(collective_id=1, has_side_effects=True),
+    )
+
+
+def make_finish(window, tile_rows, tile_cols):
+    w = window
+
+    def kernel(own, strip, low, diag, total, grad, probe):
+        r, c, m = place()
+        below, inner = r > 0, c > 0
+        first = pl.program_id(0) == 0
+        when(inner, lambda: grad.__setitem__(..., own[...] + strip[...]))
+        when(jnp.logical_not(inner), lambda: grad.__setitem__(..., own[...]))
+        when(first & below, lambda: grad.__setitem__(..., grad[...] + low[...]))
+        when(first & below & inner, lambda: grad.__setitem__(..., grad[...] + diag[...]))
+        when(first, lambda: probe.__setitem__(..., total[...]))
+
+    block = pl.BlockSpec((2, w, tile_cols), lambda i: (0, i, 0))
+    once = pl.BlockSpec((2, w, tile_cols), lambda i: (0, 0, 0))
+    return pl.pallas_call(
+        kernel,
+        name="finish",
+        grid=(tile_rows // w,),
+        in_specs=[block, block, once, once, once],
+        out_specs=[block, once],
+        out_shape=[
+            jax.ShapeDtypeStruct((2, tile_rows, tile_cols), F32),
+            jax.ShapeDtypeStruct((2, w, w), F32),
+        ],
+    )
+
+
 def per_device(object_slab, probe_modes, amplitudes, scan_counts, scan_positions):
     window = probe_modes.shape[-1]
     tile_rows, tile_cols = object_slab.shape[1:]
     slots = amplitudes.shape[0]
-    modes = lax.axis_size("mode")
-    cols_n = lax.axis_size("col")
-    rows_n = lax.axis_size("row")
-    row_id, col_id, mode_id = lax.axis_index("row"), lax.axis_index("col"), lax.axis_index("mode")
-
-    def diagonal(by):
-        pairs = []
-        for r in range(rows_n):
-            for c in range(cols_n):
-                if 0 <= r + by < rows_n and 0 <= c + by < cols_n:
-                    pairs.append((r * cols_n + c, (r + by) * cols_n + c + by))
-        return pairs
-
-    def along(axis, by):
-        n = lax.axis_size(axis)
-        return [(i, i + by) for i in range(n) if 0 <= i + by < n]
-
-    right = lax.ppermute(object_slab, "col", along("col", -1))
-    top = object_slab[:, :window, :]
-    low = lax.ppermute(top, "row", along("row", -1))
-    diag = lax.ppermute(top, ("row", "col"), diagonal(-1))
-    probe = lax.all_gather(probe_modes, "mode", axis=1, tiled=True)
-    meta = jnp.concatenate([
-        scan_positions[0] - row_id * tile_rows,
-        scan_positions[1] - col_id * tile_cols,
-        lax.dynamic_slice(scan_counts, (row_id * cols_n + col_id,), (1,)),
-        mode_id[None].astype(jnp.int32),
-    ])
+    modes, cols_n, rows_n = (lax.axis_size(a) for a in ("mode", "col", "row"))
+    sizes = (window, modes, tile_rows, tile_cols, rows_n, cols_n)
+    right, low, diag, probe = make_spread(*sizes)(object_slab, probe_modes)
     consts = [jnp.asarray(t) for t in tables(window)]
-    compute = make_compute(window, modes, slots, tile_rows, tile_cols)
+    compute = make_compute(window, modes, slots, tile_rows, tile_cols, cols_n)
     g_own, g_right, g_low, g_diag, pg, shift = compute(
-        meta, object_slab, right, low, diag, probe, amplitudes, *consts
-    )
-    from_left = lax.ppermute(g_right, "col", along("col", 1))
-    from_up = lax.ppermute(g_low, "row", along("row", 1))
-    from_diag = lax.ppermute(g_diag, ("row", "col"), diagonal(1))
-    grad = g_own + from_left
-    grad = grad.at[:, :window, :].add(from_up + from_diag)
-    probe_total = lax.psum(pg, ("row", "col"))[:, None] / 16.0
-    return (grad, probe_total, shift)
+        scan_positions, scan_counts, object_slab, right, low, diag, probe, amplitudes, *consts
+    )
+    from_left, from_up, from_diag, total = make_collect(*sizes)(
+        g_right, g_low, g_diag, pg.reshape(2 * window, window)
+    )
+    grad, probe_grad = make_finish(window, tile_rows, tile_cols)(
+        g_own, from_left, from_up, from_diag, total.reshape(2, window, window)
+    )
+    return (grad, probe_grad.reshape(2, 1, window, window), shift)
 
 
 def solution(mesh):

time: 334 us -> 199 us (0.60)
  waiting for transfers between devices: 224 us -> 0 us
  Pallas kernels: 68 us -> 198 us
  between operations: 14.1 us -> 0.65 us
  starting transfers between devices: 12.8 us -> 0 us
  other arithmetic: 8.1 us -> 0 us
  local copies, waits for them, and re-layouts: 5.12 us -> 0 us
    psum x1 -> x0, waiting for transfers between devices: 175 us -> none  [per_device(): probe_total = lax.psum(pg, ('row', 'col'))[:, None] / 16.0]
    pallas_call x1 -> x4, Pallas kernels: 68 us -> 198 us  [the longest x1 86.2 us: per_device(): compute(scan_positions, scan_counts, object_slab, right, low, diag, probe...]
    ppermute x6 -> x0, waiting for transfers between devices: 49.5 us -> none  [the longest x1 43.5 us: per_device(): diag = lax.ppermute(top, ('row', 'col'), diagonal(-1))]
    ppermute x6 -> x0, starting transfers between devices: 12.7 us -> none  [the longest x1 3.62 us: per_device(): right = lax.ppermute(object_slab, 'col', along('col', -1))]
    add x1 -> x0, other arithmetic: 4.01 us -> none  [per_device(): grad = g_own + from_left]
  transfers between devices with their start and end apart: 8 -> 0, of which waited for: 3 -> 0; matrix products, arithmetic and copies ran while one was open for 3% -> 0% of each run, Pallas kernels for 0% -> 0%
where the time goes in v3:
time: 199 us
  Pallas kernels  198 us (99%)
    pallas_call x1, Pallas kernels, per_device(): compute(scan_positions, scan_counts, object_slab, right, low, diag, probe...  86.2 us
    pallas_call x1, Pallas kernels, per_device(): make_collect(*sizes)(g_right, g_low, g_diag, pg.reshape(2 * window, window))  72.7 us
    pallas_call x1, Pallas kernels, per_device(): right, low, diag, probe = make_spread(*sizes)(object_slab, probe_modes)  31 us
    pallas_call x1, Pallas kernels, per_device(): make_finish(window, tile_rows, tile_cols)  8.41 us

profile of v3, /device:TPU:10, one launch (start us, length us, event | category | flops | bytes accessed | tf_op | source)
XLA Modules:
  0.0 199.0 jit_solution(4492526815075854366)
XLA Ops:
  0.6 31.0 %spread.1 = (f32[2,2048,256]{2,1,0:T(8,128)}, f32[2,256,256]{2,1,0:T(8,128)}, f32[2,256,256]{2,1,0:T(8,128)}, f32[2,4,256,256]{3,2,1,0:T(8,128)}) custom-call(f32[2,2048,256]{2,1,0:T(8,128)} %own.1, f32[2,1,256,256]{3,2,1,0:T(8,128)} %probe.1), custom_call_target="tpu_custom_call" | custom-call | tf_op jit(solution)/shard_map/spread/pallas_call | solution.py:678
  31.6 86.2 %slots.1 = (f32[2,2048,256]{2,1,0:T(8,128)}, f32[2,2048,256]{2,1,0:T(8,128)}, f32[2,256,256]{2,1,0:T(8,128)}, f32[2,256,256]{2,1,0:T(8,128)}, f32[2,256,256]{2,1,0:T(8,128)}, /*index=5*/f32[2,16]{1,0:T(2,128)}) custom-call(s32[2,16]{1,0:T(2,128)} %positions.1, s32[32]{0:T(128)} %counts.1, f32[2,2048,256]{2,1,0:T(8,128)} %own.1, ...), custom_call_target="tpu_custom_call" | custom-call | flops 99999997952 | bytes 10000000 | tf_op jit(solution)/shard_map/slots/pallas_call | solution.py:681
  117.9 72.7 %collect.1 = (f32[2,2048,256]{2,1,0:T(8,128)}, f32[2,256,256]{2,1,0:T(8,128)}, f32[2,256,256]{2,1,0:T(8,128)}, f32[512,256]{1,0:T(8,128)}) custom-call(f32[2,2048,256]{2,1,0:T(8,128)} %get-tuple-element.24.g_right, f32[2,256,256]{2,1,0:T(8,128)} %get-tuple-element.25.g_low, f32[2,256,256]{2,1,0:T(8,128)} %get-tuple-element.26.g_diag, f32[512,256]{1,0:T(8,128)} %bitcast.6), custom_call_target="tpu_custom_call" | custom-call | tf_op jit(solution)/shard_map/collect/pallas_call | solution.py:684
  190.6 8.4 %finish.1 = (f32[2,2048,256]{2,1,0:T(8,128)}, f32[2,256,256]{2,1,0:T(8,128)}) custom-call(f32[2,2048,256]{2,1,0:T(8,128)} %get-tuple-element.23.own, f32[2,2048,256]{2,1,0:T(8,128)} %get-tuple-element.28.strip, f32[2,256,256]{2,1,0:T(8,128)} %get-tuple-element.29.low, f32[2,256,256]{2,1,0:T(8,128)} %get-tuple-element.30.diag, f32[2,256,256]{2,1,0:T(8,128)} %bitcast.5), custom_call_target="tpu_custom_call" | custom-call | tf_op jit(solution)/shard_map/finish/pallas_call | solution.py:687

commit v4 on v3

--- a/solution.py
+++ b/solution.py
@@ -10,6 +10,8 @@
 
 BF = jnp.bfloat16
 F32 = jnp.float32
+BATCH = 4
+CH = 32
 
 
 def hi_lo(x):
@@ -18,30 +20,36 @@
     return hi, lo
 
 
+def halves(table):
+    table = table.astype(np.float32)
+    hi = table.astype(BF)
+    return hi, (table - hi.astype(np.float32)).astype(BF)
+
+
+def angles(window, radix, q):
+    part = window // radix
+    n, j = np.arange(part)[:, None], np.arange(part)[None, :]
+    angle = 2.0 * math.pi * ((n * (radix * j + q)) % window) / window
+    return np.cos(angle) / math.sqrt(window), np.sin(angle) / math.sqrt(window)
+
+
 def tables(window):
-    half = window // 2
-    n = np.arange(half)[:, None]
-    j = np.arange(half)[None, :]
-    scale = 1.0 / math.sqrt(window)
-    forward, inverse = [], []
-    for parity in range(2):
-        angle = 2.0 * math.pi * ((n * (2 * j + parity)) % window) / window
-        c, s = np.cos(angle) * scale, np.sin(angle) * scale
-        forward.append(np.block([[c, -s], [s, c]]))
-        inverse.append(np.block([[c.T, s.T], [-s.T, c.T]]))
-    sides = []
-    for axis in (1, 2):
-        for table in (np.stack(forward), np.stack(inverse)):
-            table = table.astype(np.float32)
-            if axis == 2:
-                table = np.swapaxes(table, 1, 2)
-            hi = table.astype(BF)
-            lo = (table - hi.astype(np.float32)).astype(BF)
-            sides.append(np.concatenate([hi, lo, hi], axis=axis))
+    right_f, right_i, left_f, left_i = [], [], [], []
+    for q in range(2):
+        c, s = angles(window, 2, q)
+        for table, into in ((np.block([[c, -s], [s, c]]), right_f), (np.block([[c.T, s.T], [-s.T, c.T]]), right_i)):
+            hi, lo = halves(table)
+            into.append(np.concatenate([hi, lo, hi], axis=0))
+    for q in range(4):
+        c, s = angles(window, 4, q)
+        for table, into in ((np.block([[c.T, s.T], [-s.T, c.T]]), left_f), (np.block([[c, -s], [s, c]]), left_i)):
+            hi, lo = halves(table)
+            top = np.concatenate([hi, hi], axis=1)
+            into.append(np.concatenate([top, np.concatenate([lo, np.zeros_like(lo)], axis=1)], axis=0))
     order = np.concatenate([np.arange(0, window, 2), np.arange(1, window, 2)])
     shuffle = np.zeros((window, window), np.float32)
     shuffle[order, np.arange(window)] = 1.0
-    return sides[0], sides[1], sides[2], sides[3], shuffle.astype(BF)
+    return np.stack(right_f), np.stack(right_i), np.stack(left_f), np.stack(left_i), shuffle.astype(BF)
 
 
 def cat(parts, axis):
@@ -53,8 +61,8 @@
 
 
 def make_compute(window, modes, slots, tile_rows, tile_cols, cols_n):
-    w, half = window, window // 2
-    ch = 32
+    w, half, quart = window, window // 2, window // 4
+    ch = CH
     ext_rows, ext_cols = tile_rows + w, tile_cols + w
 
     def kernel(positions, counts, own, right, low, diag, probe, amps, rf, ri, lf, li, shuffle,
@@ -107,19 +115,79 @@
         for copy in loads:
             copy.wait()
 
+        def put_lhs(parity, at, x):
+            hi, lo = hi_lo(x)
+            lhs[parity, at:at + ch, :w] = hi
+            lhs[parity, at:at + ch, w:] = lo
+
+        def put_rhs(m, q, at, x):
+            hi, lo = hi_lo(x)
+            rhs[m, q, at:at + ch, :] = hi
+            rhs[m, q, half + at:half + at + ch, :] = lo
+
+        def right_apply(m, table, into):
+            rows = slice(m * w, (m + BATCH) * w)
+            for parity in range(2):
+                hi, lo = lhs[parity, rows, :w], lhs[parity, rows, w:]
+                into[parity, rows, :] = mm(cat([hi, hi, lo], 1), table[parity])
+
+        def left_apply(m, q, table):
+            both = mm(table[q], rhs[m, q])
+            return both[:half] + both[half:]
+
+        def forward_rows(m):
+            for r in range(0, quart, ch):
+                y = [[], [], [], []]
+                for parity in range(2):
+                    x = [mid[parity, m * w + p * quart + r:m * w + p * quart + r + ch, :] for p in range(4)]
+                    a, b, c, d = x[0] + x[2], x[1] + x[3], x[0] - x[2], x[1] - x[3]
+                    y[0].append(a + b)
+                    y[2].append(a - b)
+                    turned = cat([d[:, half:], -d[:, :half]], 1)
+                    y[1].append(c + turned)
+                    y[3].append(c - turned)
+                for q in range(4):
+                    e, o = y[q]
+                    put_rhs(m, q, r, cat([e[:, :half], o[:, :half]], 1))
+                    put_rhs(m, q, quart + r, cat([e[:, half:], o[:, half:]], 1))
+            for q in range(4):
+                far[m, q] = left_apply(m, q, lf)
+
+        def inverse_rows(m):
+            for q in range(4):
+                for r in range(0, quart, ch):
+                    f = fac[q, r:r + ch, :]
+                    for at in (r, quart + r):
+                        put_rhs(m, q, at, f * far[m, q, at:at + ch, :])
+            for q in range(4):
+                far[m, q] = left_apply(m, q, li)
+            for r in range(0, quart, ch):
+                re = [far[m, q, r:r + ch, :] for q in range(4)]
+                im = [far[m, q, quart + r:quart + r + ch, :] for q in range(4)]
+                are, aim, bre, bim = re[0] + re[2], im[0] + im[2], re[1] + re[3], im[1] + im[3]
+                cre, cim, dre, dim = re[0] - re[2], im[0] - im[2], re[1] - re[3], im[1] - im[3]
+                outs = (
+                    (are + bre, aim + bim), (cre - dim, cim + dre),
+                    (are - bre, aim - bim), (cre + dim, cim - dre),
+                )
+                for p, (xre, xim) in enumerate(outs):
+                    for parity in range(2):
+                        cols = slice(parity * half, parity * half + half)
+                        put_lhs(parity, m * w + p * quart + r, cat([xre[:, cols], xim[:, cols]], 1))
+
         def do_slot(slot, carry):
             row = positions[0, slot] - row_id * tile_rows
             col = positions[1, slot] - col_id * tile_cols
             tile_at = col // 128
             off = lax.rem(col, 128)
             back = lax.rem(w + 128 - off, w + 128)
-            place = lax.rem(slot, 2)
-            for copy in amp_copies(slot, place):
+            place_at = lax.rem(slot, 2)
+            for copy in amp_copies(slot, place_at):
                 copy.wait()
 
             @pl.when(slot + 1 < count)
             def _():
-                for copy in amp_copies(slot + 1, 1 - place):
+                for copy in amp_copies(slot + 1, 1 - place_at):
                     copy.start()
 
             for c in range(2):
@@ -127,13 +195,12 @@
                     wide = cat([ext[tile_at + t, c, pl.ds(row + r, ch), :] for t in range(3)], 1)
                     win[c, r:r + ch, :] = pltpu.roll(wide, back, 1)[:, :w]
 
-            for parity in range(2):
-                a = cat([amp_buf[place, t, pl.ds(parity, half, stride=2), :] for t in range(2)], 1)
-                a0, rest = a.astype(BF), None
-                r1 = a - a0.astype(F32)
-                a1 = r1.astype(BF)
-                a2 = (r1 - a1.astype(F32)).astype(BF)
-                fac[parity] = mm(a0, shuffle[...]) + mm(a1, shuffle[...]) + mm(a2, shuffle[...])
+            for q in range(4):
+                a = cat([amp_buf[place_at, t, pl.ds(q, quart, stride=4), :] for t in range(2)], 1)
+                a0, a1 = hi_lo(a)
+                a2 = (a - a0.astype(F32) - a1.astype(F32)).astype(BF)
+                stack = mm(cat([a0, a1, a2], 0), shuffle[...])
+                fac[q] = stack[:quart] + stack[quart:2 * quart] + stack[2 * quart:]
 
             for m in range(modes):
                 for r in range(0, w, ch):
@@ -146,70 +213,26 @@
                             x = cat([are[:, :half] + are[:, half:], aim[:, :half] + aim[:, half:]], 1)
                         else:
                             x = cat([are[:, :half] - are[:, half:], aim[:, :half] - aim[:, half:]], 1)
-                        hi, lo = hi_lo(x)
-                        lhs[m, parity, r:r + ch, :w] = hi
-                        lhs[m, parity, r:r + ch, w:] = lo
-                for parity in range(2):
-                    hi, lo = lhs[m, parity, :, :w], lhs[m, parity, :, w:]
-                    mid[m, parity] = mm(cat([hi, hi, lo], 1), rf[parity])
-                for r in range(0, half, ch):
-                    e_top, e_bot = mid[m, 0, r:r + ch, :], mid[m, 0, half + r:half + r + ch, :]
-                    o_top, o_bot = mid[m, 1, r:r + ch, :], mid[m, 1, half + r:half + r + ch, :]
-                    for parity in range(2):
-                        if parity == 0:
-                            e, o = e_top + e_bot, o_top + o_bot
-                        else:
-                            e, o = e_top - e_bot, o_top - o_bot
-                        hi, lo = hi_lo(cat([e[:, :half], o[:, :half]], 1))
-                        rhs[m, parity, 0, r:r + ch, :] = hi
-                        rhs[m, parity, 1, r:r + ch, :] = lo
-                        hi, lo = hi_lo(cat([e[:, half:], o[:, half:]], 1))
-                        rhs[m, parity, 0, half + r:half + r + ch, :] = hi
-                        rhs[m, parity, 1, half + r:half + r + ch, :] = lo
-                for parity in range(2):
-                    hi, lo = rhs[m, parity, 0], rhs[m, parity, 1]
-                    far[m, parity] = mm(lf[parity], cat([hi, hi, lo], 0))
-
-            for parity in range(2):
-                for r in range(0, half, ch):
+                        put_lhs(parity, m * w + r, x)
+                if (m + 1) % BATCH == 0:
+                    right_apply(m + 1 - BATCH, rf, mid)
+                    for n in range(m + 1 - BATCH, m + 1):
+                        forward_rows(n)
+
+            for q in range(4):
+                for r in range(0, quart, ch):
                     total = None
                     for m in range(modes):
-                        re = far[m, parity, r:r + ch, :]
-                        im = far[m, parity, half + r:half + r + ch, :]
+                        re = far[m, q, r:r + ch, :]
+                        im = far[m, q, quart + r:quart + r + ch, :]
                         term = re * re + im * im
                         total = term if total is None else total + term
-                    f = 0.25 * (1.0 - fac[parity, r:r + ch, :] * lax.rsqrt(total + 0.5))
-                    fac[parity, r:r + ch, :] = f
+                    fac[q, r:r + ch, :] = 0.25 * (1.0 - fac[q, r:r + ch, :] * lax.rsqrt(total + 0.5))
 
             for m in range(modes):
-                for parity in range(2):
-                    for r in range(0, half, ch):
-                        f = fac[parity, r:r + ch, :]
-                        for part in range(2):
-                            at = part * half + r
-                            hi, lo = hi_lo(f * far[m, parity, at:at + ch, :])
-                            rhs[m, parity, 0, at:at + ch, :] = hi
-                            rhs[m, parity, 1, at:at + ch, :] = lo
-                for parity in range(2):
-                    hi, lo = rhs[m, parity, 0], rhs[m, parity, 1]
-                    mid[m, parity] = mm(li[parity], cat([hi, hi, lo], 0))
-                for r in range(0, half, ch):
-                    e_re, e_im = mid[m, 0, r:r + ch, :], mid[m, 0, half + r:half + r + ch, :]
-                    o_re, o_im = mid[m, 1, r:r + ch, :], mid[m, 1, half + r:half + r + ch, :]
-                    for top in range(2):
-                        if top == 0:
-                            re, im = e_re + o_re, e_im + o_im
-                        else:
-                            re, im = e_re - o_re, e_im - o_im
-                        at = top * half + r
-                        for parity in range(2):
-                            cols = slice(parity * half, parity * half + half)
-                            hi, lo = hi_lo(cat([re[:, cols], im[:, cols]], 1))
-                            lhs[m, parity, at:at + ch, :w] = hi
-                            lhs[m, parity, at:at + ch, w:] = lo
-                for parity in range(2):
-                    hi, lo = lhs[m, parity, :, :w], lhs[m, parity, :, w:]
-                    near[m, parity] = mm(cat([hi, hi, lo], 1), ri[parity])
+                inverse_rows(m)
+                if (m + 1) % BATCH == 0:
+                    right_apply(m + 1 - BATCH, ri, near)
 
             rows_sum = jnp.zeros((8, w), F32)
             cols_sum = jnp.zeros((8, w), F32)
@@ -217,7 +240,10 @@
             inner = (lanes >= 1) & (lanes <= w - 2)
 
             def near_of(m, r):
-                e, o = near[m, 0, pl.ds(r, ch), :], near[m, 1, pl.ds(r, ch), :]
+                at = m * w + r
+                if not isinstance(m, int):
+                    at = pl.multiple_of(at, ch)
+                e, o = near[0, pl.ds(at, ch), :], near[1, pl.ds(at, ch), :]
                 s, d = e + o, e - o
                 return cat([s[:, :half], d[:, :half]], 1), cat([s[:, half:], d[:, half:]], 1)
 
@@ -293,12 +319,12 @@
             pltpu.VMEM((ext_cols // 128, 2, ext_rows, 128), F32),
             pltpu.VMEM((2, 2, w, 128), F32),
             pltpu.VMEM((2, w, w), F32),
-            pltpu.VMEM((2, half, w), F32),
-            pltpu.VMEM((modes, 2, w, 2 * w), BF),
-            pltpu.VMEM((modes, 2, 2, w, w), BF),
-            pltpu.VMEM((modes, 2, w, w), F32),
-            pltpu.VMEM((modes, 2, w, w), F32),
-            pltpu.VMEM((modes, 2, w, w), F32),
+            pltpu.VMEM((4, quart, w), F32),
+            pltpu.VMEM((2, modes * w, 2 * w), BF),
+            pltpu.VMEM((modes, 4, w, w), BF),
+            pltpu.VMEM((2, modes * w, w), F32),
+            pltpu.VMEM((modes, 4, half, w), F32),
+            pltpu.VMEM((2, modes * w, w), F32),
             pltpu.SemaphoreType.DMA((2, 2)),
             pltpu.SemaphoreType.DMA((8,)),
         ],
@@ -437,21 +463,36 @@
         corner_on = remote(low, diag, one_s.at[1], one_r.at[1], device(r, other, m))
 
         def probe_copy(k):
-            half = gathered.at[pl.ds(core, 1), pl.ds(m, 1)]
-            return remote(
-                probe.at[pl.ds(core, 1)], half, p_s.at[k], p_r.at[k], device(r, c, lax.rem(m + k, modes))
-            )
+            to = device(r, c, lax.rem(m + k, modes))
+            return remote(probe, gathered.at[:, pl.ds(m, 1)], p_s.at[k], p_r.at[k], to)
 
         def probe_pass(k):
-            half = gathered.at[pl.ds(core, 1), pl.ds(lax.rem(m + modes - k, modes), 1)]
-            return remote(half, half, x_s.at[k], x_r.at[k], device(r, other, m))
+            one = gathered.at[:, pl.ds(lax.rem(m + modes - k, modes), 1)]
+            return remote(one, one, x_s.at[k], x_r.at[k], device(r, other, m))
+
+        def probe_start():
+            for k in far:
+                probe_copy(k).start()
+
+        def probe_turn():
+            for k in far:
+                probe_copy(k).wait_recv()
+                probe_pass(k).start()
+
+        def probe_finish():
+            for k in far:
+                probe_pass(k).wait_send()
+                probe_copy(k).wait_send()
+
+        def probe_take():
+            for k in far:
+                probe_pass(k).wait_recv()
 
         far = (1, modes - 1, 2)
         when(even & has_away, strip.start)
         when(r == 1, down.start)
         when(even & has_diag, corner.start)
-        for k in far:
-            probe_copy(k).start()
+        when(even, probe_start)
         when(odd, whole.start)
         keep = pltpu.make_async_copy(probe, gathered.at[:, pl.ds(m, 1)], own_sem)
         keep.start()
@@ -465,17 +506,13 @@
         when(odd & has_away, strip.turn)
         when(r == 0, down.finish)
         when(odd & (r == 0), corner_on.start)
-        for k in far:
-            probe_copy(k).wait_recv()
-            probe_pass(k).start()
+        when(even, probe_turn)
         when(odd & has_diag, corner.finish)
         when(odd & has_away, strip.finish)
         when(even, whole.wait_recv)
         when(even & (r == 0), corner_on.wait_recv)
-        for k in far:
-            probe_pass(k).wait_recv()
-            probe_pass(k).wait_send()
-            probe_copy(k).wait_send()
+        when(odd, probe_take)
+        when(even, probe_finish)
         keep.wait()
         when(odd, whole.wait_send)
         when(odd & (r == 0), corner_on.wait_send)
@@ -506,7 +543,7 @@
 def make_collect(window, modes, tile_rows, tile_cols, rows_n, cols_n):
     w = window
     chips = rows_n * cols_n // 2
-    piece = w // chips
+    piece = 2 * w // chips
 
     def kernel(g_right, g_low, g_diag, pg, right, low, diag, total, *sems):
         strip_sems, low_sems, diag_sems = sems[:6], sems[6:12], sems[12:18]
@@ -530,92 +567,87 @@
             greet(partner(k))
             return carry
 
-        lax.fori_loop(1, chips, hello, 0)
         greet(device(r, other, m))
         for k in (1, modes - 1):
             greet(device(r, c, lax.rem(m + k, modes)))
         when(has_away, lambda: greet(device(r, away, m)))
         when(has_over, lambda: greet(device(flip, over, m)))
+        when(even, lambda: greet(device(flip, c, m)))
+        when(odd, lambda: lax.fori_loop(1, chips, hello, 0))
         pl.semaphore_wait(
             pltpu.get_barrier_semaphore(),
-            chips + 2 + has_away.astype(jnp.int32) + has_over.astype(jnp.int32),
+            3 + jnp.where(odd, chips - 1, 1) + has_away.astype(jnp.int32) + has_over.astype(jnp.int32),
         )
 
         strip = Quarters(g_right, right, modes, tile_rows, r, away, STRIP, strip_sems)
         down = Quarters(g_low, low, modes, w, flip, c, EDGE, low_sems)
         corner = Quarters(g_diag, diag, modes, w, flip, over, EDGE, diag_sems)
         whole = remote(g_right, right, one_s, one_r, device(r, other, m))
-        my_half = pl.ds(pl.multiple_of(core * w, w), w)
-        its_half = pl.ds(pl.multiple_of((1 - core) * w, w), w)
-
-        swap = remote(pg.at[its_half, :], pair.at[0], x_s, x_r, device(r, other, m))
-        swap.start()
-        own = pltpu.make_async_copy(pg.at[my_half, :], pair.at[1], in_sem)
-        own.start()
+        swap = remote(pg, pair.at[0], x_s, x_r, device(r, other, m))
+        own = pltpu.make_async_copy(pg, pair.at[1], in_sem)
+        at_chip = pl.ds(pl.multiple_of(chip * piece, piece), piece)
+        rest = got.at[pl.ds(1, chips - 1)]
+        many = total.at[pl.ds(0, (chips - 1) * piece), :]
+        keep = pltpu.make_async_copy(mine, total.at[at_chip, :], in_sem)
+        give = remote(total, total, y_s, y_r, device(r, other, m))
+
+        def scatter_go(k, carry):
+            p = lax.rem(chip + k, chips)
+            rows = pl.ds(pl.multiple_of(p * piece, piece), piece)
+            remote(pair.at[1, rows, :], got.at[k], a_s, a_r, partner(k)).start()
+            return carry
+
+        def share_go(k, carry):
+            remote(mine, total.at[at_chip, :], b_s, b_r, partner(k)).start()
+            return carry
+
+        def add(k, acc):
+            return acc + got[k]
+
+        def sum_pair():
+            own.wait()
+            swap.wait_recv()
+            pair[1] = pair[0] + pair[1]
+            lax.fori_loop(1, chips, scatter_go, 0)
+
+        def sum_plane():
+            pltpu.make_async_copy(rest, rest, a_r).wait()
+            mine[...] = lax.fori_loop(1, chips, add, pair[1, at_chip, :]) * (1.0 / 16.0)
+            keep.start()
+            lax.fori_loop(1, chips, share_go, 0)
+
+        def sum_give():
+            keep.wait()
+            pltpu.make_async_copy(many, many, b_r).wait()
+            give.start()
+
+        def sum_end():
+            pltpu.make_async_copy(rest, rest, a_s).wait()
+            pltpu.make_async_copy(many, many, b_s).wait()
+            give.wait_send()
+
+        when(even, swap.start)
+        when(odd, own.start)
         when(odd & has_away, strip.start)
         when(r == 0, down.start)
         when((r == 0) & has_over, corner.start)
-
-        own.wait()
-        swap.wait_recv()
-        pair[1] = pair[0] + pair[1]
         when(even, whole.start)
-
-        def scatter(k):
-            p = lax.rem(chip + k, chips)
-            rows = pl.ds(pl.multiple_of(p * piece, piece), piece)
-            return remote(pair.at[1, rows, :], got.at[k], a_s, a_r, partner(k))
-
-        def scatter_go(k, carry):
-            scatter(k).start()
-            return carry
-
-        lax.fori_loop(1, chips, scatter_go, 0)
-        when(even & has_away, lambda: strip.take([0]))
+        when(odd, sum_pair)
+        when(even & has_away, strip.take)
         when(r == 1, down.take)
         when((r == 1) & has_over, corner.take)
-
-        rest = got.at[pl.ds(1, chips - 1)]
-        pltpu.make_async_copy(rest, rest, a_r).wait()
-        at_chip = pl.ds(pl.multiple_of(chip * piece, piece), piece)
-
-        def add(k, acc):
-            return acc + got[k]
-
-        mine[...] = lax.fori_loop(1, chips, add, pair[1, at_chip, :]) * (1.0 / 16.0)
-        at_me = pl.ds(pl.multiple_of(core * w + chip * piece, piece), piece)
-
-        def share(k):
-            return remote(mine, total.at[at_me, :], b_s, b_r, partner(k))
-
-        def share_go(k, carry):
-            share(k).start()
-            return carry
-
-        keep = pltpu.make_async_copy(mine, total.at[at_me, :], in_sem)
-        keep.start()
-        lax.fori_loop(1, chips, share_go, 0)
-
-        when(even & has_away, lambda: strip.take([1, 2, 3]))
+        when(odd, sum_plane)
+        when(even & has_away, strip.turn)
         when(r == 1, down.turn)
         when((r == 1) & has_over, corner.turn)
-        when(even & has_away, strip.turn)
-
-        keep.wait()
-        many = total.at[pl.ds(0, (chips - 1) * piece), :]
-        pltpu.make_async_copy(many, many, b_r).wait()
-        give = remote(total.at[my_half, :], total.at[my_half, :], y_s, y_r, device(r, other, m))
-        give.start()
-
+        when(odd, sum_give)
+        when(even & has_away, strip.finish)
         when(r == 1, down.finish)
         when((r == 1) & has_over, corner.finish)
-        when(even & has_away, strip.finish)
         when(odd, whole.wait_recv)
-        give.wait_recv()
-        give.wait_send()
-        swap.wait_send()
-        pltpu.make_async_copy(rest, rest, a_s).wait()
-        pltpu.make_async_copy(many, many, b_s).wait()
+        when(even, give.wait_recv)
+        when(even, swap.wait_send)
+        when(odd, sum_end)
         when(odd & has_away, strip.sent)
         when(r == 0, down.sent)
         when((r == 0) & has_over, corner.sent)
@@ -636,7 +668,7 @@
             shape((2 * w, w), F32),
         ],
         scratch_shapes=quarter_sems(STRIP) + quarter_sems(EDGE) + quarter_sems(EDGE) + [dma] * 11
-        + [pltpu.VMEM((2, w, w), F32), pltpu.VMEM((chips, piece, w), F32), pltpu.VMEM((piece, w), F32)],
+        + [pltpu.VMEM((2, 2 * w, w), F32), pltpu.VMEM((chips, piece, w), F32), pltpu.VMEM((piece, w), F32)],
         compiler_params=pltpu.CompilerParams(collective_id=1, has_side_effects=True),
     )
 

time: 199 us -> 167 us (0.84)
  Pallas kernels: 198 us -> 165 us
    pallas_call x1, Pallas kernels: 86.2 us -> 23.9 us  [per_device(): compute(scan_positions, scan_counts, object_slab, right, low, diag, probe...]
    pallas_call x1, Pallas kernels: 72.7 us -> 107 us  [per_device(): make_collect(*sizes)(g_right, g_low, g_diag, pg.reshape(2 * window, window))]
    pallas_call x1, Pallas kernels: 31 us -> 25.4 us  [per_device(): right, low, diag, probe = make_spread(*sizes)(object_slab, probe_modes)]
where the time goes in v4:
time: 167 us; the launch traced here: 165 us
  Pallas kernels  165 us (99%)
    pallas_call x1, Pallas kernels, per_device(): make_collect(*sizes)(g_right, g_low, g_diag, pg.reshape(2 * window, window))  107 us
    pallas_call x1, Pallas kernels, per_device(): right, low, diag, probe = make_spread(*sizes)(object_slab, probe_modes)  25.4 us
    pallas_call x1, Pallas kernels, per_device(): compute(scan_positions, scan_counts, object_slab, right, low, diag, probe...  23.9 us
    pallas_call x1, Pallas kernels, per_device(): make_finish(window, tile_rows, tile_cols)  8.41 us

profile of v4, /device:TPU:10, one launch (start us, length us, event | category | flops | bytes accessed | tf_op | source)
XLA Modules:
  0.0 165.5 jit_solution(1242122356879513407)
XLA Ops:
  0.6 25.4 %spread.1 = (f32[2,2048,256]{2,1,0:T(8,128)}, f32[2,256,256]{2,1,0:T(8,128)}, f32[2,256,256]{2,1,0:T(8,128)}, f32[2,4,256,256]{3,2,1,0:T(8,128)}) custom-call(f32[2,2048,256]{2,1,0:T(8,128)} %own.1, f32[2,1,256,256]{3,2,1,0:T(8,128)} %probe.1), custom_call_target="tpu_custom_call" | custom-call | tf_op jit(solution)/shard_map/spread/pallas_call | solution.py:710
  26.1 23.9 %slots.1 = (f32[2,2048,256]{2,1,0:T(8,128)}, f32[2,2048,256]{2,1,0:T(8,128)}, f32[2,256,256]{2,1,0:T(8,128)}, f32[2,256,256]{2,1,0:T(8,128)}, f32[2,256,256]{2,1,0:T(8,128)}, /*index=5*/f32[2,16]{1,0:T(2,128)}) custom-call(s32[2,16]{1,0:T(2,128)} %positions.1, s32[32]{0:T(128)} %counts.1, f32[2,2048,256]{2,1,0:T(8,128)} %own.1, ...), custom_call_target="tpu_custom_call" | custom-call | flops 99999997952 | bytes 10000000 | tf_op jit(solution)/shard_map/slots/pallas_call | solution.py:713
  49.9 107.1 %collect.1 = (f32[2,2048,256]{2,1,0:T(8,128)}, f32[2,256,256]{2,1,0:T(8,128)}, f32[2,256,256]{2,1,0:T(8,128)}, f32[512,256]{1,0:T(8,128)}) custom-call(f32[2,2048,256]{2,1,0:T(8,128)} %get-tuple-element.24.g_right, f32[2,256,256]{2,1,0:T(8,128)} %get-tuple-element.25.g_low, f32[2,256,256]{2,1,0:T(8,128)} %get-tuple-element.26.g_diag, f32[512,256]{1,0:T(8,128)} %bitcast.6), custom_call_target="tpu_custom_call" | custom-call | tf_op jit(solution)/shard_map/collect/pallas_call | solution.py:716
  157.1 8.4 %finish.1 = (f32[2,2048,256]{2,1,0:T(8,128)}, f32[2,256,256]{2,1,0:T(8,128)}) custom-call(f32[2,2048,256]{2,1,0:T(8,128)} %get-tuple-element.23.own, f32[2,2048,256]{2,1,0:T(8,128)} %get-tuple-element.28.strip, f32[2,256,256]{2,1,0:T(8,128)} %get-tuple-element.29.low, f32[2,256,256]{2,1,0:T(8,128)} %get-tuple-element.30.diag, f32[2,256,256]{2,1,0:T(8,128)} %bitcast.5), custom_call_target="tpu_custom_call" | custom-call | tf_op jit(solution)/shard_map/finish/pallas_call | solution.py:719

commit v5 on v4

--- a/solution.py
+++ b/solution.py
@@ -355,9 +355,9 @@
 
 
 class Quarters:
-    def __init__(self, src, dst, modes, rows, r, c, chunks, sems):
+    def __init__(self, src, dst, modes, rows, r, c, chunks, sems, direct=False):
         me_r, me_c, m = place()
-        self.m, self.modes, self.chunks = m, modes, chunks
+        self.m, self.modes, self.chunks, self.direct = m, modes, chunks, direct
         self.rows = rows // modes // chunks
         self.src, self.dst = src, dst
         self.ys, self.yr, self.zs, self.zr, self.ts, self.tr = sems
@@ -385,13 +385,23 @@
         block = self.part(self.dst, lax.rem(self.m + back, self.modes), i)
         return remote(block, block, self.ts.at[i], self.tr.at[i], self.next if self.way(i) == 0 else self.prev)
 
+    def second(self, i):
+        owner = lax.rem(self.m + self.modes // 2, self.modes)
+        return remote(
+            self.part(self.src, owner, i), self.part(self.dst, owner, i), self.ts.at[i], self.tr.at[i], self.peer
+        )
+
     def start(self):
         for i in range(self.chunks):
             self.first(i).start()
+        for i in range(self.chunks) if self.direct else ():
+            self.second(i).start()
 
     def sent(self):
         for i in range(self.chunks):
             self.first(i).wait_send()
+            if self.direct:
+                self.second(i).wait_send()
 
     def take(self, some=None):
         for i in range(self.chunks) if some is None else some:
@@ -402,16 +412,21 @@
     def turn(self):
         for i in range(self.chunks):
             self.ring(i, self.way(i)).wait_recv()
-            self.relay(i).start()
+            if not self.direct:
+                self.relay(i).start()
 
     def finish(self):
         for i in range(self.chunks):
             self.ring(i, 1 - self.way(i)).wait_recv()
-            self.relay(i).wait_recv()
+            if self.direct:
+                self.second(i).wait_recv()
+            else:
+                self.relay(i).wait_recv()
         for i in range(self.chunks):
             self.ring(i, 0).wait_send()
             self.ring(i, 1).wait_send()
-            self.relay(i).wait_send()
+            if not self.direct:
+                self.relay(i).wait_send()
 
 
 STRIP, EDGE = 4, 2
@@ -456,33 +471,49 @@
             modes + 1 + has_away.astype(jnp.int32) + has_diag.astype(jnp.int32),
         )
 
-        strip = Quarters(tile, right, modes, tile_rows, r, away, STRIP, strip_sems)
+        strip = Quarters(tile, right, modes, tile_rows, r, away, STRIP, strip_sems, True)
         down = Quarters(tile, low, modes, w, flip, c, EDGE, low_sems)
         corner = Quarters(tile, diag, modes, w, flip, away, EDGE, diag_sems)
         whole = remote(tile, right, one_s.at[0], one_r.at[0], device(r, other, m))
         corner_on = remote(low, diag, one_s.at[1], one_r.at[1], device(r, other, m))
 
+        def probe_of(k, part=None):
+            parts = pl.ds(0, 2) if part is None else pl.ds(part, 1)
+            return gathered.at[parts, pl.ds(lax.rem(m + modes - k, modes), 1)]
+
         def probe_copy(k):
             to = device(r, c, lax.rem(m + k, modes))
-            return remote(probe, gathered.at[:, pl.ds(m, 1)], p_s.at[k], p_r.at[k], to)
+            return remote(probe, probe_of(0), p_s.at[k], p_r.at[k], to)
+
+        def probe_relay(k):
+            block = probe_of(k, 0 if k == 1 else 1)
+            at = 0 if k == 1 else 2
+            return remote(block, block, p_s.at[at], p_r.at[at], device(r, c, lax.rem(m + k, modes)))
 
         def probe_pass(k):
-            one = gathered.at[:, pl.ds(lax.rem(m + modes - k, modes), 1)]
-            return remote(one, one, x_s.at[k], x_r.at[k], device(r, other, m))
+            return remote(probe_of(k), probe_of(k), x_s.at[k], x_r.at[k], device(r, other, m))
 
         def probe_start():
-            for k in far:
+            for k in (1, modes - 1):
                 probe_copy(k).start()
 
         def probe_turn():
-            for k in far:
+            for k in (1, modes - 1):
                 probe_copy(k).wait_recv()
+                probe_relay(k).start()
                 probe_pass(k).start()
 
+        def probe_end():
+            for k in (1, modes - 1):
+                probe_relay(k).wait_recv()
+            probe_pass(2).start()
+
         def probe_finish():
+            for k in (1, modes - 1):
+                probe_copy(k).wait_send()
+                probe_relay(k).wait_send()
             for k in far:
                 probe_pass(k).wait_send()
-                probe_copy(k).wait_send()
 
         def probe_take():
             for k in far:
@@ -498,6 +529,7 @@
         keep.start()
 
         when(odd & has_away, lambda: strip.take([0]))
+        when(even, probe_turn)
         when(r == 0, down.take)
         when(odd & has_diag, corner.take)
         when(odd & has_away, lambda: strip.take([1, 2, 3]))
@@ -506,7 +538,7 @@
         when(odd & has_away, strip.turn)
         when(r == 0, down.finish)
         when(odd & (r == 0), corner_on.start)
-        when(even, probe_turn)
+        when(even, probe_end)
         when(odd & has_diag, corner.finish)
         when(odd & has_away, strip.finish)
         when(even, whole.wait_recv)
@@ -675,29 +707,63 @@
 
 def make_finish(window, tile_rows, tile_cols):
     w = window
-
-    def kernel(own, strip, low, diag, total, grad, probe):
+    blocks = tile_rows // w
+
+    def kernel(own, strip, low, diag, total, grad, probe, a, b, e, s_a, s_b, s_e, s_out):
         r, c, m = place()
         below, inner = r > 0, c > 0
-        first = pl.program_id(0) == 0
-        when(inner, lambda: grad.__setitem__(..., own[...] + strip[...]))
-        when(jnp.logical_not(inner), lambda: grad.__setitem__(..., own[...]))
-        when(first & below, lambda: grad.__setitem__(..., grad[...] + low[...]))
-        when(first & below & inner, lambda: grad.__setitem__(..., grad[...] + diag[...]))
-        when(first, lambda: probe.__setitem__(..., total[...]))
-
-    block = pl.BlockSpec((2, w, tile_cols), lambda i: (0, i, 0))
-    once = pl.BlockSpec((2, w, tile_cols), lambda i: (0, 0, 0))
+
+        def rows(k):
+            return pl.ds(k * w, w)
+
+        loads = [
+            [
+                pltpu.make_async_copy(own.at[:, rows(k), :], a.at[:, rows(k), :], s_a.at[k]),
+                pltpu.make_async_copy(strip.at[:, rows(k), :], b.at[:, rows(k), :], s_b.at[k]),
+            ]
+            for k in range(blocks)
+        ]
+        edges = [pltpu.make_async_copy(src, e.at[n], s_e.at[n]) for n, src in enumerate((low, diag, total))]
+        for k in reversed(range(blocks)):
+            for copy in loads[k]:
+                copy.start()
+        for copy in edges:
+            copy.start()
+        stores = [pltpu.make_async_copy(a.at[:, rows(k), :], grad.at[:, rows(k), :], s_out.at[k]) for k in range(blocks)]
+
+        def add(k, x):
+            for part in range(2):
+                a[part, k * w:k * w + w, :] += x[part]
+
+        for k in reversed(range(blocks)):
+            for copy in loads[k]:
+                copy.wait()
+            when(inner, lambda: add(k, b.at[:, rows(k), :]))
+            if k == 0:
+                for copy in edges:
+                    copy.wait()
+                when(below, lambda: add(0, e.at[0]))
+                when(below & inner, lambda: add(0, e.at[1]))
+                last = pltpu.make_async_copy(e.at[2], probe, s_out.at[blocks])
+                last.start()
+            stores[k].start()
+        for copy in stores + [last]:
+            copy.wait()
+
+    hbm = pl.BlockSpec(memory_space=pl.ANY)
+    dma = pltpu.SemaphoreType.DMA
+    tile = (2, tile_rows, tile_cols)
     return pl.pallas_call(
         kernel,
         name="finish",
-        grid=(tile_rows // w,),
-        in_specs=[block, block, once, once, once],
-        out_specs=[block, once],
-        out_shape=[
-            jax.ShapeDtypeStruct((2, tile_rows, tile_cols), F32),
-            jax.ShapeDtypeStruct((2, w, w), F32),
+        in_specs=[hbm] * 5,
+        out_specs=[hbm] * 2,
+        out_shape=[jax.ShapeDtypeStruct(tile, F32), jax.ShapeDtypeStruct((2, w, w), F32)],
+        scratch_shapes=[
+            pltpu.VMEM(tile, F32), pltpu.VMEM(tile, F32), pltpu.VMEM((3, 2, w, w), F32),
+            dma((blocks,)), dma((blocks,)), dma((3,)), dma((blocks + 1,)),
         ],
+        compiler_params=pltpu.CompilerParams(vmem_limit_bytes=40 << 20),
     )
 
 

time: 167 us -> 180 us (1.078)
  local copies, waits for them, and re-layouts: 0 us -> 7.49 us
  Pallas kernels: 165 us -> 172 us
    pallas_call x1, Pallas kernels: 23.9 us -> 37.1 us  [per_device(): compute(scan_positions, scan_counts, object_slab, right, low, diag, probe...]
    unnamed x0 -> x10, local copies, waits for them, and re-layouts: none -> 7.49 us
    pallas_call x1, Pallas kernels: 107 us -> 101 us  [per_device(): make_collect(*sizes)(g_right, g_low, g_diag, pg.reshape(2 * window, window))]
    pallas_call x1, Pallas kernels: 8.41 us -> 3.16 us  [per_device(): make_finish(window, tile_rows, tile_cols)]
    pallas_call x1, Pallas kernels: 25.4 us -> 30.4 us  [per_device(): right, low, diag, probe = make_spread(*sizes)(object_slab, probe_modes)]
where the time goes in v5:
time: 180 us
  Pallas kernels  172 us (96%)
  local copies, waits for them, and re-layouts  7.49 us (4%)
    pallas_call x1, Pallas kernels, per_device(): make_collect(*sizes)(g_right, g_low, g_diag, pg.reshape(2 * window, window))  101 us
    pallas_call x1, Pallas kernels, per_device(): compute(scan_positions, scan_counts, object_slab, right, low, diag, probe...  37.1 us
    pallas_call x1, Pallas kernels, per_device(): right, low, diag, probe = make_spread(*sizes)(object_slab, probe_modes)  30.4 us
    unnamed x10, local copies, waits for them, and re-layouts  7.49 us

profile of v5, /device:TPU:10, one launch (start us, length us, event | category | flops | bytes accessed | tf_op | source)
XLA Modules:
  0.0 179.9 jit_solution(18346109238928141871)
XLA Ops:
  0.6 30.4 %spread.1 = (f32[2,2048,256]{2,1,0:T(8,128)}, f32[2,256,256]{2,1,0:T(8,128)}, f32[2,256,256]{2,1,0:T(8,128)}, f32[2,4,256,256]{3,2,1,0:T(8,128)}) custom-call(f32[2,2048,256]{2,1,0:T(8,128)} %own.1, f32[2,1,256,256]{3,2,1,0:T(8,128)} %probe.1), custom_call_target="tpu_custom_call" | custom-call | tf_op jit(solution)/shard_map/spread/pallas_call | solution.py:776
  31.1 37.1 %slots.1 = (f32[2,2048,256]{2,1,0:T(8,128)}, f32[2,2048,256]{2,1,0:T(8,128)}, f32[2,256,256]{2,1,0:T(8,128)}, f32[2,256,256]{2,1,0:T(8,128)}, f32[2,256,256]{2,1,0:T(8,128)}, /*index=5*/f32[2,16]{1,0:T(2,128)}) custom-call(s32[2,16]{1,0:T(2,128)} %positions.1, s32[32]{0:T(128)} %counts.1, f32[2,2048,256]{2,1,0:T(8,128)} %own.1, ...), custom_call_target="tpu_custom_call" | custom-call | flops 99999997952 | bytes 10000000 | tf_op jit(solution)/shard_map/slots/pallas_call | solution.py:779
  68.2 101.0 %collect.1 = (f32[2,2048,256]{2,1,0:T(8,128)}, f32[2,256,256]{2,1,0:T(8,128)}, f32[2,256,256]{2,1,0:T(8,128)}, f32[512,256]{1,0:T(8,128)}) custom-call(f32[2,2048,256]{2,1,0:T(8,128)} %get-tuple-element.24.g_right, f32[2,256,256]{2,1,0:T(8,128)} %get-tuple-element.25.g_low, f32[2,256,256]{2,1,0:T(8,128)} %get-tuple-element.26.g_diag, f32[512,256]{1,0:T(8,128)} %bitcast.6), custom_call_target="tpu_custom_call" | custom-call | tf_op jit(solution)/shard_map/collect/pallas_call | solution.py:782
  169.2 0.0 copy-start
  169.3 2.2 %copy-done = f32[2,2048,256]{2,1,0:T(8,128)S(1)} copy-done((f32[2,2048,256]{2,1,0:T(8,128)S(1)}, f32[2,2048,256]{2,1,0:T(8,128)}, u32[]{:S(2)}) %copy-start) | copy-done | bytes 4194328
  171.4 0.0 copy-start.1
  171.4 2.2 %copy-done.1 = f32[2,2048,256]{2,1,0:T(8,128)S(1)} copy-done((f32[2,2048,256]{2,1,0:T(8,128)S(1)}, f32[2,2048,256]{2,1,0:T(8,128)}, u32[]{:S(2)}) %copy-start.1) | copy-done | bytes 4194328
  173.6 0.0 copy-start.2
  173.6 1.0 copy-done.2
  174.7 0.0 copy-start.3
  174.7 1.0 copy-done.3
  175.7 0.0 copy-start.4
  175.7 1.0 copy-done.4
  176.7 3.2 %finish.1 = (f32[2,2048,256]{2,1,0:T(8,128)}, f32[2,256,256]{2,1,0:T(8,128)}) custom-call(f32[2,2048,256]{2,1,0:T(8,128)S(1)} %copy-done, f32[2,2048,256]{2,1,0:T(8,128)S(1)} %copy-done.1, f32[2,256,256]{2,1,0:T(8,128)S(1)} %copy-done.2, f32[2,256,256]{2,1,0:T(8,128)S(1)} %copy-done.3, f32[2,256,256]{2,1,0:T(8,128)S(1)} %bitcast.5), custom_call_target="tpu_custom_call" | custom-call | tf_op jit(solution)/shard_map/finish/pallas_call | solution.py:785
Async XLA Ops:
  169.2 2.2 %copy-start = (f32[2,2048,256]{2,1,0:T(8,128)S(1)}, f32[2,2048,256]{2,1,0:T(8,128)}, u32[]{:S(2)}) copy-start(f32[2,2048,256]{2,1,0:T(8,128)} %get-tuple-element.23.own) | copy-start | bytes 12582916
  171.4 2.2 %copy-start.1 = (f32[2,2048,256]{2,1,0:T(8,128)S(1)}, f32[2,2048,256]{2,1,0:T(8,128)}, u32[]{:S(2)}) copy-start(f32[2,2048,256]{2,1,0:T(8,128)} %get-tuple-element.28.strip) | copy-start | bytes 12582916
  173.6 1.0 copy-start.2
  174.7 1.0 copy-start.3
  175.7 1.0 copy-start.4

commit v6 on v5

--- a/solution.py
+++ b/solution.py
@@ -520,24 +520,24 @@
                 probe_pass(k).wait_recv()
 
         far = (1, modes - 1, 2)
-        when(even & has_away, strip.start)
         when(r == 1, down.start)
         when(even & has_diag, corner.start)
+        when(even & has_away, strip.start)
         when(even, probe_start)
         when(odd, whole.start)
         keep = pltpu.make_async_copy(probe, gathered.at[:, pl.ds(m, 1)], own_sem)
         keep.start()
 
-        when(odd & has_away, lambda: strip.take([0]))
-        when(even, probe_turn)
         when(r == 0, down.take)
         when(odd & has_diag, corner.take)
-        when(odd & has_away, lambda: strip.take([1, 2, 3]))
+        when(odd & has_away, lambda: strip.take([0]))
         when(r == 0, down.turn)
         when(odd & has_diag, corner.turn)
-        when(odd & has_away, strip.turn)
+        when(even, probe_turn)
+        when(odd & has_away, lambda: strip.take([1, 2, 3]))
         when(r == 0, down.finish)
         when(odd & (r == 0), corner_on.start)
+        when(odd & has_away, strip.turn)
         when(even, probe_end)
         when(odd & has_diag, corner.finish)
         when(odd & has_away, strip.finish)
@@ -660,18 +660,19 @@
 
         when(even, swap.start)
         when(odd, own.start)
-        when(odd & has_away, strip.start)
         when(r == 0, down.start)
         when((r == 0) & has_over, corner.start)
+        when(odd & has_away, strip.start)
         when(even, whole.start)
         when(odd, sum_pair)
-        when(even & has_away, strip.take)
         when(r == 1, down.take)
         when((r == 1) & has_over, corner.take)
-        when(odd, sum_plane)
-        when(even & has_away, strip.turn)
+        when(even & has_away, lambda: strip.take([0]))
         when(r == 1, down.turn)
         when((r == 1) & has_over, corner.turn)
+        when(odd, sum_plane)
+        when(even & has_away, lambda: strip.take([1, 2, 3]))
+        when(even & has_away, strip.turn)
         when(odd, sum_give)
         when(even & has_away, strip.finish)
         when(r == 1, down.finish)
@@ -763,7 +764,7 @@
             pltpu.VMEM(tile, F32), pltpu.VMEM(tile, F32), pltpu.VMEM((3, 2, w, w), F32),
             dma((blocks,)), dma((blocks,)), dma((3,)), dma((blocks + 1,)),
         ],
-        compiler_params=pltpu.CompilerParams(vmem_limit_bytes=40 << 20),
+        compiler_params=pltpu.CompilerParams(vmem_limit_bytes=60 << 20),
     )
 
 

time: 180 us -> 176 us (0.978)
  the two profiles are of different devices: /device:TPU:10 before, /device:TPU:24 now
where the time goes in v6:
time: 176 us; the launch traced here: 174 us
  Pallas kernels  173 us (98%)
    pallas_call x1, Pallas kernels, per_device(): compute(scan_positions, scan_counts, object_slab, right, low, diag, probe...  81.4 us
    pallas_call x1, Pallas kernels, per_device(): make_collect(*sizes)(g_right, g_low, g_diag, pg.reshape(2 * window, window))  54.9 us
    pallas_call x1, Pallas kernels, per_device(): right, low, diag, probe = make_spread(*sizes)(object_slab, probe_modes)  30.4 us
    pallas_call x1, Pallas kernels, per_device(): make_finish(window, tile_rows, tile_cols)  6.29 us

profile of v6, /device:TPU:24, one launch (start us, length us, event | category | flops | bytes accessed | tf_op | source)
XLA Modules:
  0.0 173.7 jit_solution(5833358467506657231)
XLA Ops:
  0.6 30.4 %spread.1 = (f32[2,2048,256]{2,1,0:T(8,128)}, f32[2,256,256]{2,1,0:T(8,128)}, f32[2,256,256]{2,1,0:T(8,128)}, f32[2,4,256,256]{3,2,1,0:T(8,128)}) custom-call(f32[2,2048,256]{2,1,0:T(8,128)} %own.1, f32[2,1,256,256]{3,2,1,0:T(8,128)} %probe.1), custom_call_target="tpu_custom_call" | custom-call | tf_op jit(solution)/shard_map/spread/pallas_call | solution.py:777
  31.1 81.4 %slots.1 = (f32[2,2048,256]{2,1,0:T(8,128)}, f32[2,2048,256]{2,1,0:T(8,128)}, f32[2,256,256]{2,1,0:T(8,128)}, f32[2,256,256]{2,1,0:T(8,128)}, f32[2,256,256]{2,1,0:T(8,128)}, /*index=5*/f32[2,16]{1,0:T(2,128)}) custom-call(s32[2,16]{1,0:T(2,128)} %positions.1, s32[32]{0:T(128)} %counts.1, f32[2,2048,256]{2,1,0:T(8,128)} %own.1, ...), custom_call_target="tpu_custom_call" | custom-call | flops 99999997952 | bytes 10000000 | tf_op jit(solution)/shard_map/slots/pallas_call | solution.py:780
  112.5 54.9 %collect.1 = (f32[2,2048,256]{2,1,0:T(8,128)}, f32[2,256,256]{2,1,0:T(8,128)}, f32[2,256,256]{2,1,0:T(8,128)}, f32[512,256]{1,0:T(8,128)}) custom-call(f32[2,2048,256]{2,1,0:T(8,128)} %get-tuple-element.24.g_right, f32[2,256,256]{2,1,0:T(8,128)} %get-tuple-element.25.g_low, f32[2,256,256]{2,1,0:T(8,128)} %get-tuple-element.26.g_diag, f32[512,256]{1,0:T(8,128)} %bitcast.6), custom_call_target="tpu_custom_call" | custom-call | tf_op jit(solution)/shard_map/collect/pallas_call | solution.py:783
  167.4 6.3 %finish.1 = (f32[2,2048,256]{2,1,0:T(8,128)}, f32[2,256,256]{2,1,0:T(8,128)}) custom-call(f32[2,2048,256]{2,1,0:T(8,128)} %get-tuple-element.23.own, f32[2,2048,256]{2,1,0:T(8,128)} %get-tuple-element.28.strip, f32[2,256,256]{2,1,0:T(8,128)} %get-tuple-element.29.low, f32[2,256,256]{2,1,0:T(8,128)} %get-tuple-element.30.diag, f32[2,256,256]{2,1,0:T(8,128)} %bitcast.5), custom_call_target="tpu_custom_call" | custom-call | tf_op jit(solution)/shard_map/finish/pallas_call | solution.py:786

commit v7 on v6

--- a/solution.py
+++ b/solution.py
@@ -355,9 +355,9 @@
 
 
 class Quarters:
-    def __init__(self, src, dst, modes, rows, r, c, chunks, sems, direct=False):
+    def __init__(self, src, dst, modes, rows, r, c, chunks, sems, held=False):
         me_r, me_c, m = place()
-        self.m, self.modes, self.chunks, self.direct = m, modes, chunks, direct
+        self.m, self.modes, self.chunks, self.held = m, modes, chunks, held
         self.rows = rows // modes // chunks
         self.src, self.dst = src, dst
         self.ys, self.yr, self.zs, self.zr, self.ts, self.tr = sems
@@ -370,7 +370,7 @@
         return ref.at[:, pl.ds(at, self.rows), :]
 
     def first(self, i):
-        mine = self.part(self.src, self.m, i)
+        mine = self.part(self.src, 0 if self.held else self.m, i)
         return remote(mine, self.part(self.dst, self.m, i), self.ys.at[i], self.yr.at[i], self.peer)
 
     def ring(self, i, way):
@@ -385,23 +385,13 @@
         block = self.part(self.dst, lax.rem(self.m + back, self.modes), i)
         return remote(block, block, self.ts.at[i], self.tr.at[i], self.next if self.way(i) == 0 else self.prev)
 
-    def second(self, i):
-        owner = lax.rem(self.m + self.modes // 2, self.modes)
-        return remote(
-            self.part(self.src, owner, i), self.part(self.dst, owner, i), self.ts.at[i], self.tr.at[i], self.peer
-        )
-
     def start(self):
         for i in range(self.chunks):
             self.first(i).start()
-        for i in range(self.chunks) if self.direct else ():
-            self.second(i).start()
 
     def sent(self):
         for i in range(self.chunks):
             self.first(i).wait_send()
-            if self.direct:
-                self.second(i).wait_send()
 
     def take(self, some=None):
         for i in range(self.chunks) if some is None else some:
@@ -412,21 +402,16 @@
     def turn(self):
         for i in range(self.chunks):
             self.ring(i, self.way(i)).wait_recv()
-            if not self.direct:
-                self.relay(i).start()
+            self.relay(i).start()
 
     def finish(self):
         for i in range(self.chunks):
             self.ring(i, 1 - self.way(i)).wait_recv()
-            if self.direct:
-                self.second(i).wait_recv()
-            else:
-                self.relay(i).wait_recv()
+            self.relay(i).wait_recv()
         for i in range(self.chunks):
             self.ring(i, 0).wait_send()
             self.ring(i, 1).wait_send()
-            if not self.direct:
-                self.relay(i).wait_send()
+            self.relay(i).wait_send()
 
 
 STRIP, EDGE = 4, 2
@@ -450,14 +435,13 @@
 
     def kernel(tile, probe, right, low, diag, gathered, *sems):
         strip_sems, low_sems, diag_sems = sems[:6], sems[6:12], sems[12:18]
-        one_s, one_r, p_s, p_r, x_s, x_r, own_sem = sems[18:]
+        one_s, one_r, p_s, p_r, x_s, x_r, h_s, h_r, own_sem, held = sems[18:]
         r, c, m = place()
         core = lax.rem(c, 2)
         other = c + 1 - 2 * core
         odd, even = core == 1, core == 0
         away = jnp.where(odd, jnp.minimum(c + 1, cols_n - 1), jnp.maximum(c - 1, 0))
         has_away = jnp.where(odd, c < cols_n - 1, c > 0)
-        has_diag = has_away & jnp.where(odd, r == 0, r == 1)
         flip = rows_n - 1 - r
 
         for k in range(1, modes):
@@ -465,15 +449,13 @@
         greet(device(r, other, m))
         greet(device(flip, c, m))
         when(has_away, lambda: greet(device(r, away, m)))
-        when(has_diag, lambda: greet(device(flip, away, m)))
-        pl.semaphore_wait(
-            pltpu.get_barrier_semaphore(),
-            modes + 1 + has_away.astype(jnp.int32) + has_diag.astype(jnp.int32),
-        )
-
-        strip = Quarters(tile, right, modes, tile_rows, r, away, STRIP, strip_sems, True)
+        pl.semaphore_wait(pltpu.get_barrier_semaphore(), modes + 1 + has_away.astype(jnp.int32))
+
+        strip = Quarters(tile, right, modes, tile_rows, r, away, STRIP, strip_sems)
         down = Quarters(tile, low, modes, w, flip, c, EDGE, low_sems)
-        corner = Quarters(tile, diag, modes, w, flip, away, EDGE, diag_sems)
+        corner = Quarters(held, diag, modes, w, flip, c, EDGE, diag_sems, True)
+        top = tile.at[:, pl.ds(pl.multiple_of(m * (w // modes), w // modes), w // modes), :]
+        hop = remote(top, held, h_s, h_r, device(r, away, m))
         whole = remote(tile, right, one_s.at[0], one_r.at[0], device(r, other, m))
         corner_on = remote(low, diag, one_s.at[1], one_r.at[1], device(r, other, m))
 
@@ -520,26 +502,27 @@
                 probe_pass(k).wait_recv()
 
         far = (1, modes - 1, 2)
+        when((r == 1) & even & has_away, hop.start)
         when(r == 1, down.start)
-        when(even & has_diag, corner.start)
         when(even & has_away, strip.start)
         when(even, probe_start)
         when(odd, whole.start)
         keep = pltpu.make_async_copy(probe, gathered.at[:, pl.ds(m, 1)], own_sem)
         keep.start()
 
+        when((r == 1) & odd & has_away, hop.wait_recv, corner.start)
         when(r == 0, down.take)
-        when(odd & has_diag, corner.take)
+        when((r == 0) & odd & has_away, corner.take)
         when(odd & has_away, lambda: strip.take([0]))
         when(r == 0, down.turn)
-        when(odd & has_diag, corner.turn)
+        when((r == 0) & odd & has_away, corner.turn)
         when(even, probe_turn)
         when(odd & has_away, lambda: strip.take([1, 2, 3]))
         when(r == 0, down.finish)
         when(odd & (r == 0), corner_on.start)
         when(odd & has_away, strip.turn)
         when(even, probe_end)
-        when(odd & has_diag, corner.finish)
+        when((r == 0) & odd & has_away, corner.finish)
         when(odd & has_away, strip.finish)
         when(even, whole.wait_recv)
         when(even & (r == 0), corner_on.wait_recv)
@@ -550,7 +533,8 @@
         when(odd & (r == 0), corner_on.wait_send)
         when(even & has_away, strip.sent)
         when(r == 1, down.sent)
-        when(even & has_diag, corner.sent)
+        when((r == 1) & even & has_away, hop.wait_send)
+        when((r == 1) & odd & has_away, corner.sent)
 
     hbm = pl.BlockSpec(memory_space=pl.ANY)
     shape = jax.ShapeDtypeStruct
@@ -567,7 +551,8 @@
             shape((2, modes, w, w), F32),
         ],
         scratch_shapes=quarter_sems(STRIP) + quarter_sems(EDGE) + quarter_sems(EDGE)
-        + [dma((2,))] * 2 + [dma((modes,))] * 4 + [dma],
+        + [dma((2,))] * 2 + [dma((modes,))] * 4 + [dma] * 3
+        + [pltpu.VMEM((2, w // modes, tile_cols), F32)],
         compiler_params=pltpu.CompilerParams(collective_id=0, has_side_effects=True),
     )
 
@@ -579,7 +564,7 @@
 
     def kernel(g_right, g_low, g_diag, pg, right, low, diag, total, *sems):
         strip_sems, low_sems, diag_sems = sems[:6], sems[6:12], sems[12:18]
-        one_s, one_r, x_s, x_r, y_s, y_r, a_s, a_r, b_s, b_r, in_sem, pair, got, mine = sems[18:]
+        one_s, one_r, x_s, x_r, y_s, y_r, a_s, a_r, b_s, b_r, h_s, h_r, in_sem, pair, got, mine, held = sems[18:]
         r, c, m = place()
         core = lax.rem(c, 2)
         chip = r * (cols_n // 2) + c // 2
@@ -588,8 +573,6 @@
         away = jnp.where(odd, jnp.minimum(c + 1, cols_n - 1), jnp.maximum(c - 1, 0))
         has_away = jnp.where(odd, c < cols_n - 1, c > 0)
         flip = rows_n - 1 - r
-        over = jnp.where(r == 0, jnp.minimum(c + 1, cols_n - 1), jnp.maximum(c - 1, 0))
-        has_over = jnp.where(r == 0, c < cols_n - 1, c > 0)
 
         def partner(k):
             p = lax.rem(chip + k, chips)
@@ -603,17 +586,18 @@
         for k in (1, modes - 1):
             greet(device(r, c, lax.rem(m + k, modes)))
         when(has_away, lambda: greet(device(r, away, m)))
-        when(has_over, lambda: greet(device(flip, over, m)))
         when(even, lambda: greet(device(flip, c, m)))
         when(odd, lambda: lax.fori_loop(1, chips, hello, 0))
         pl.semaphore_wait(
             pltpu.get_barrier_semaphore(),
-            3 + jnp.where(odd, chips - 1, 1) + has_away.astype(jnp.int32) + has_over.astype(jnp.int32),
+            3 + jnp.where(odd, chips - 1, 1) + has_away.astype(jnp.int32),
         )
 
         strip = Quarters(g_right, right, modes, tile_rows, r, away, STRIP, strip_sems)
         down = Quarters(g_low, low, modes, w, flip, c, EDGE, low_sems)
-        corner = Quarters(g_diag, diag, modes, w, flip, over, EDGE, diag_sems)
+        corner = Quarters(held, diag, modes, w, flip, c, EDGE, diag_sems, True)
+        top = g_diag.at[:, pl.ds(pl.multiple_of(m * (w // modes), w // modes), w // modes), :]
+        hop = remote(top, held, h_s, h_r, device(r, jnp.minimum(c + 1, cols_n - 1), m))
         whole = remote(g_right, right, one_s, one_r, device(r, other, m))
         swap = remote(pg, pair.at[0], x_s, x_r, device(r, other, m))
         own = pltpu.make_async_copy(pg, pair.at[1], in_sem)
@@ -660,30 +644,32 @@
 
         when(even, swap.start)
         when(odd, own.start)
+        when((r == 0) & (c < cols_n - 1), hop.start)
         when(r == 0, down.start)
-        when((r == 0) & has_over, corner.start)
+        when((r == 0) & (c > 0), hop.wait_recv, corner.start)
         when(odd & has_away, strip.start)
         when(even, whole.start)
         when(odd, sum_pair)
         when(r == 1, down.take)
-        when((r == 1) & has_over, corner.take)
+        when((r == 1) & (c > 0), corner.take)
         when(even & has_away, lambda: strip.take([0]))
         when(r == 1, down.turn)
-        when((r == 1) & has_over, corner.turn)
+        when((r == 1) & (c > 0), corner.turn)
         when(odd, sum_plane)
         when(even & has_away, lambda: strip.take([1, 2, 3]))
         when(even & has_away, strip.turn)
         when(odd, sum_give)
         when(even & has_away, strip.finish)
         when(r == 1, down.finish)
-        when((r == 1) & has_over, corner.finish)
+        when((r == 1) & (c > 0), corner.finish)
         when(odd, whole.wait_recv)
         when(even, give.wait_recv)
         when(even, swap.wait_send)
         when(odd, sum_end)
         when(odd & has_away, strip.sent)
         when(r == 0, down.sent)
-        when((r == 0) & has_over, corner.sent)
+        when((r == 0) & (c < cols_n - 1), hop.wait_send)
+        when((r == 0) & (c > 0), corner.sent)
         when(even, whole.wait_send)
 
     hbm = pl.BlockSpec(memory_space=pl.ANY)
@@ -700,8 +686,8 @@
             shape((2, w, tile_cols), F32),
             shape((2 * w, w), F32),
         ],
-        scratch_shapes=quarter_sems(STRIP) + quarter_sems(EDGE) + quarter_sems(EDGE) + [dma] * 11
-        + [pltpu.VMEM((2, 2 * w, w), F32), pltpu.VMEM((chips, piece, w), F32), pltpu.VMEM((piece, w), F32)],
+        scratch_shapes=quarter_sems(STRIP) + quarter_sems(EDGE) + quarter_sems(EDGE) + [dma] * 13
+        + [pltpu.VMEM((2, 2 * w, w), F32), pltpu.VMEM((chips, piece, w), F32), pltpu.VMEM((piece, w), F32), pltpu.VMEM((2, w // modes, w), F32)],
         compiler_params=pltpu.CompilerParams(collective_id=1, has_side_effects=True),
     )
 

time: 176 us -> 170 us (0.966)
  the two profiles are of different devices: /device:TPU:24 before, /device:TPU:26 now
where the time goes in v7:
time: 170 us; the launch traced here: 168 us
  Pallas kernels  167 us (98%)
    pallas_call x1, Pallas kernels, per_device(): make_collect(*sizes)(g_right, g_low, g_diag, pg.reshape(2 * window, window))  122 us
    pallas_call x1, Pallas kernels, per_device(): right, low, diag, probe = make_spread(*sizes)(object_slab, probe_modes)  23.8 us
    pallas_call x1, Pallas kernels, per_device(): compute(scan_positions, scan_counts, object_slab, right, low, diag, probe...  15.1 us
    pallas_call x1, Pallas kernels, per_device(): make_finish(window, tile_rows, tile_cols)  6.29 us

profile of v7, /device:TPU:26, one launch (start us, length us, event | category | flops | bytes accessed | tf_op | source)
XLA Modules:
  0.0 167.5 jit_solution(7920227527692661417)
XLA Ops:
  0.6 23.8 %spread.1 = (f32[2,2048,256]{2,1,0:T(8,128)}, f32[2,256,256]{2,1,0:T(8,128)}, f32[2,256,256]{2,1,0:T(8,128)}, f32[2,4,256,256]{3,2,1,0:T(8,128)}) custom-call(f32[2,2048,256]{2,1,0:T(8,128)} %own.1, f32[2,1,256,256]{3,2,1,0:T(8,128)} %probe.1), custom_call_target="tpu_custom_call" | custom-call | tf_op jit(solution)/shard_map/spread/pallas_call | solution.py:763
  24.4 15.1 %slots.1 = (f32[2,2048,256]{2,1,0:T(8,128)}, f32[2,2048,256]{2,1,0:T(8,128)}, f32[2,256,256]{2,1,0:T(8,128)}, f32[2,256,256]{2,1,0:T(8,128)}, f32[2,256,256]{2,1,0:T(8,128)}, /*index=5*/f32[2,16]{1,0:T(2,128)}) custom-call(s32[2,16]{1,0:T(2,128)} %positions.1, s32[32]{0:T(128)} %counts.1, f32[2,2048,256]{2,1,0:T(8,128)} %own.1, ...), custom_call_target="tpu_custom_call" | custom-call | flops 99999997952 | bytes 10000000 | tf_op jit(solution)/shard_map/slots/pallas_call | solution.py:766
  39.5 121.7 %collect.1 = (f32[2,2048,256]{2,1,0:T(8,128)}, f32[2,256,256]{2,1,0:T(8,128)}, f32[2,256,256]{2,1,0:T(8,128)}, f32[512,256]{1,0:T(8,128)}) custom-call(f32[2,2048,256]{2,1,0:T(8,128)} %get-tuple-element.24.g_right, f32[2,256,256]{2,1,0:T(8,128)} %get-tuple-element.25.g_low, f32[2,256,256]{2,1,0:T(8,128)} %get-tuple-element.26.g_diag, f32[512,256]{1,0:T(8,128)} %bitcast.6), custom_call_target="tpu_custom_call" | custom-call | tf_op jit(solution)/shard_map/collect/pallas_call | solution.py:769
  161.2 6.3 %finish.1 = (f32[2,2048,256]{2,1,0:T(8,128)}, f32[2,256,256]{2,1,0:T(8,128)}) custom-call(f32[2,2048,256]{2,1,0:T(8,128)} %get-tuple-element.23.own, f32[2,2048,256]{2,1,0:T(8,128)} %get-tuple-element.28.strip, f32[2,256,256]{2,1,0:T(8,128)} %get-tuple-element.29.low, f32[2,256,256]{2,1,0:T(8,128)} %get-tuple-element.30.diag, f32[2,256,256]{2,1,0:T(8,128)} %bitcast.5), custom_call_target="tpu_custom_call" | custom-call | tf_op jit(solution)/shard_map/finish/pallas_call | solution.py:772
